TPU v7x, 256 devices: a whole 4x4x8 slice. The times are simulated.
256 devices in a mesh: seq: 16 (over x, y), head: 16 (over z, core).
Axes of the slice: x: 4, y: 4, z: 8, core: 2. Of those that a mesh axis runs over, the one named last changes fastest.
Arguments:
- queries: bfloat16 [16384, 4096], P('seq', 'head'), may hold values from -100 to 100
- states: bfloat16 [4096, 8192], P('seq', 'head'), may hold values from -6 to 6
- key_weight: bfloat16 [8192, 4096], P(None, 'head'), may hold values from -0.0625 to 0.0625
- value_weight: bfloat16 [8192, 4096], P(None, 'head'), may hold values from -0.0625 to 0.0625
- neighbour_ids: int32 [256, 2], P('seq'), may hold values from 0 to 31, all different within a row
- out_grad: bfloat16 [16384, 4096], P('seq', 'head'), may hold values from -4 to 4
Outputs:
- context: bfloat16 [16384, 4096], P('seq', 'head')
- query_grad: bfloat16 [16384, 4096], P('seq', 'head')
- key_weight_grad: float32 [8192, 4096], P('seq', 'head')
- value_weight_grad: float32 [8192, 4096], P('seq', 'head')
Inputs may be any that keep to these rules, and one draw needn't show every extreme that they name: `neighbour_ids`: each span names 2 different pool blocks, and every block is named by some span.
All inputs are finite; a program needn't handle non-finite values.
Results may differ from a plain program's by a relative error of at most 0.04.
Values may be sent and summed in bfloat16 or wider, within the bound.
A program may use at most 128 MiB of HBM per device.

v0:
```python
import math

import jax
import jax.numpy as jnp
from jax import lax
from jax.sharding import PartitionSpec as P

HD = 128
SPAN = 64
NBR = 128
TOPN = 2


def local(queries, states, key_weight, value_weight, neighbour_ids, out_grad):
    head_cols = queries.shape[1]
    heads_here = head_cols // HD
    own_rows = states.shape[0]
    seq_count = lax.axis_size("seq")
    pool_total = own_rows * seq_count
    block_count = pool_total // NBR
    span_count = neighbour_ids.shape[0]
    score_scale = 1.0 / math.sqrt(HD)
    full_states = lax.all_gather(states, "head", axis=1, tiled=True)
    own_keys = jnp.dot(full_states, key_weight, preferred_element_type=jnp.float32).astype(
        jnp.bfloat16
    )
    own_values = jnp.dot(full_states, value_weight, preferred_element_type=jnp.float32).astype(
        jnp.bfloat16
    )
    pool_keys, pool_values = (
        lax.all_gather(own_keys, "seq", axis=0, tiled=True),
        lax.all_gather(own_values, "seq", axis=0, tiled=True),
    )
    key_rows = pool_keys.reshape(block_count, NBR, head_cols)[neighbour_ids]
    key_rows = key_rows.reshape(span_count, TOPN * NBR, heads_here, HD)
    value_rows = pool_values.reshape(block_count, NBR, head_cols)[neighbour_ids]
    value_rows = value_rows.reshape(span_count, TOPN * NBR, heads_here, HD)
    queries_here = queries.reshape(span_count, SPAN, heads_here, HD)
    grad_here = out_grad.reshape(span_count, SPAN, heads_here, HD)
    scores = (
        jnp.einsum("cqhd,ckhd->chqk", queries_here, key_rows, preferred_element_type=jnp.float32)
        * score_scale
    )
    soft_weights = jax.nn.softmax(scores, axis=-1)
    weights_low = soft_weights.astype(jnp.bfloat16)
    context = jnp.einsum(
        "chqk,ckhd->cqhd", weights_low, value_rows, preferred_element_type=jnp.float32
    ).astype(jnp.bfloat16)
    prob_grad = jnp.einsum(
        "cqhd,ckhd->chqk", grad_here, value_rows, preferred_element_type=jnp.float32
    )
    row_delta = jnp.sum(soft_weights * prob_grad, axis=-1, keepdims=True)
    score_grad = (soft_weights * (prob_grad - row_delta) * score_scale).astype(jnp.bfloat16)
    query_grad = jnp.einsum(
        "chqk,ckhd->cqhd", score_grad, key_rows, preferred_element_type=jnp.float32
    ).astype(jnp.bfloat16)
    key_part = jnp.einsum(
        "chqk,cqhd->ckhd", score_grad, queries_here, preferred_element_type=jnp.float32
    )
    value_part = jnp.einsum(
        "chqk,cqhd->ckhd", weights_low, grad_here, preferred_element_type=jnp.float32
    )
    both_parts = jnp.concatenate(
        [
            key_part.reshape(span_count * TOPN, NBR, head_cols),
            value_part.reshape(span_count * TOPN, NBR, head_cols),
        ],
        axis=2,
    )
    parts_high = both_parts.astype(jnp.bfloat16)
    parts_rest = (both_parts - parts_high.astype(jnp.float32)).astype(jnp.bfloat16)
    flat_ids = neighbour_ids.reshape(-1)
    block_range = jnp.arange(own_rows * lax.axis_size("seq") // NBR, dtype=jnp.int32)
    block_picks = (flat_ids[:, None] == block_range[None, :]).astype(jnp.bfloat16)
    summed_rows = jnp.einsum(
        "jb,jrc->brc", block_picks, parts_high, preferred_element_type=jnp.float32
    )
    summed_rows = summed_rows + jnp.einsum(
        "jb,jrc->brc", block_picks, parts_rest, preferred_element_type=jnp.float32
    )
    own_grad = lax.psum_scatter(
        summed_rows.reshape(own_rows * lax.axis_size("seq"), 2 * head_cols).astype(jnp.bfloat16),
        "seq",
        scatter_dimension=0,
        tiled=True,
    )
    weight_grads_all = lax.psum_scatter(
        jnp.einsum("rf,rc->fc", full_states, own_grad, preferred_element_type=jnp.float32).astype(
            jnp.bfloat16
        ),
        "seq",
        scatter_dimension=0,
        tiled=True,
    ).astype(jnp.float32)
    return (
        context.reshape(span_count * SPAN, head_cols),
        query_grad.reshape(span_count * SPAN, head_cols),
        weight_grads_all[:, :head_cols],
        weight_grads_all[:, head_cols:],
    )


def solution(mesh):
    in_specs = (
        P("seq", "head"),
        P("seq", "head"),
        P(None, "head"),
        P(None, "head"),
        P("seq", None),
        P("seq", "head"),
    )
    out_specs = (P("seq", "head"), P("seq", "head"), P("seq", "head"), P("seq", "head"))
    return jax.shard_map(local, mesh=mesh, in_specs=in_specs, out_specs=out_specs, check_vma=False)
```

profile of v0, /device:TPU:2, one launch (start us, length us, event | category | flops | bytes accessed | tf_op | source)
XLA Modules:
  0.0 437.8 jit_solution(14851394914533141190)
XLA Ops:
  7.9 47.0 %all-gather.4.cloned.1.call-done = bf16[256,8192]{1,0:T(8,128)(2,1)} async-done(((bf16[256,512]{1,0:T(8,128)(2,1)}), bf16[256,8192]{1,0:T(8,128)(2,1)}) %all-gather.4.cloned.1.call-update) | async-done | bytes 4194320 | tf_op jit(solution)/shard_map/all_gather | solution.py:23
  55.0 5.4 %convolution_convert_fusion.1 = bf16[256,256]{1,0:T(8,128)(2,1)} fusion(bf16[256,8192]{1,0:T(8,128)(2,1)} %all-gather.4.cloned.1.call-done, bf16[8192,256]{1,0:T(8,128)(2,1)} %param.8), kind=kOutput, calls=%fused_computation.36 | convolution fusion | flops 1073807360 | bytes 8519680 | tf_op jit(solution)/shard_map/dot_general | solution.py:24
  60.4 5.4 %convolution_convert_fusion.2 = bf16[256,256]{1,0:T(8,128)(2,1)} fusion(bf16[256,8192]{1,0:T(8,128)(2,1)} %all-gather.4.cloned.1.call-done, bf16[8192,256]{1,0:T(8,128)(2,1)} %param.9), kind=kOutput, calls=%fused_computation.37 | convolution fusion | flops 1073807360 | bytes 8519680 | tf_op jit(solution)/shard_map/dot_general | solution.py:27
  66.8 41.9 %all-gather.8.cloned.1.call-done = bf16[4096,256]{1,0:T(8,128)(2,1)} async-done(((bf16[256,256]{1,0:T(8,128)(2,1)}), bf16[4096,256]{1,0:T(8,128)(2,1)}) %all-gather.8.cloned.1.call-update) | async-done | bytes 2097168 | tf_op jit(solution)/shard_map/all_gather | solution.py:31
  108.7 3.6 gather_fusion.1
  112.3 2.5 reshape.78
  114.9 46.3 %all-gather.6.cloned.1.call-done = bf16[4096,256]{1,0:T(8,128)(2,1)} async-done(((bf16[256,256]{1,0:T(8,128)(2,1)}), bf16[4096,256]{1,0:T(8,128)(2,1)}) %all-gather.6.cloned.1.call-update) | async-done | bytes 2097168 | tf_op jit(solution)/shard_map/all_gather | solution.py:32
  161.1 3.6 gather_fusion
  164.7 4.0 reshape.77
  169.6 1.8 fusion.64
  172.7 2.2 fusion.19
  174.8 8.5 %convolution_bitcast_fusion = f32[16,256,2,128]{3,1,2,0:T(8,128)} fusion(bf16[16,64,2,128]{3,2,1,0:T(2,128)(2,1)S(1)} %reshape.50, f32[16,2,64]{2,1,0:T(2,128)S(1)} %get-tuple-element.18, f32[16,2,256,64]{2,3,1,0:T(8,128)} %copy-done.3), kind=kOutput, calls=%fused_computation.12 | convolution fusion | flops 136841472 | bytes 6823936 | tf_op jit(solution)/shard_map/chqk,cqhd->ckhd/dot_general | solution.py:60
  183.3 17.6 %convolution_bitcast_fusion.1 = f32[16,256,2,128]{3,1,2,0:T(8,128)} fusion(f32[16,2,256,64]{2,3,1,0:T(8,128)} %fusion.19, bf16[16,64,2,128]{3,2,1,0:T(2,128)(2,1)S(1)} %reshape.48, f32[16,2,64,256]{3,2,1,0:T(8,128)} %get-tuple-element.19, f32[16,2,64]{2,1,0:T(2,128)S(1)} %get-tuple-element.18), kind=kOutput, calls=%fused_computation.13 | convolution fusion | flops 137890048 | bytes 8921088 | tf_op jit(solution)/shard_map/chqk,cqhd->ckhd/dot_general | solution.py:57
  200.9 5.5 %copy.50 = f32[16,256,2,128]{1,0,3,2:T(8,128)} copy(f32[16,256,2,128]{3,1,2,0:T(8,128)} %convolution_bitcast_fusion.1) | data formatting | bytes 8388608 | tf_op jit(solution)/shard_map/chqk,cqhd->ckhd/transpose | solution.py:57
  206.4 4.7 %reshape.52 = f32[32,128,256]{1,0,2:T(8,128)} reshape(f32[16,256,2,128]{1,0,3,2:T(8,128)} %copy.50) | data formatting | bytes 8388608 | tf_op jit(solution)/shard_map/reshape | solution.py:65
  211.1 5.6 %copy.53 = f32[32,128,256]{2,0,1:T(8,128)} copy(f32[32,128,256]{1,0,2:T(8,128)} %reshape.52) | data formatting | bytes 8388608 | tf_op jit(solution)/shard_map/reshape | solution.py:65
  216.7 5.5 %copy.52 = f32[16,256,2,128]{1,0,3,2:T(8,128)} copy(f32[16,256,2,128]{3,1,2,0:T(8,128)} %convolution_bitcast_fusion) | data formatting | bytes 8388608 | tf_op jit(solution)/shard_map/chqk,cqhd->ckhd/transpose | solution.py:60
  222.2 4.7 %reshape.53 = f32[32,128,256]{1,0,2:T(8,128)} reshape(f32[16,256,2,128]{1,0,3,2:T(8,128)} %copy.52) | data formatting | bytes 8388608 | tf_op jit(solution)/shard_map/reshape | solution.py:66
  226.9 5.6 %copy.54 = f32[32,128,256]{2,0,1:T(8,128)} copy(f32[32,128,256]{1,0,2:T(8,128)} %reshape.53) | data formatting | bytes 8388608 | tf_op jit(solution)/shard_map/reshape | solution.py:66
  232.5 4.8 %fusion.4 = f32[32,128,512]{2,0,1:T(8,128)S(1)} fusion(f32[32,128,256]{2,0,1:T(8,128)} %copy.54, f32[32,128,256]{2,0,1:T(8,128)} %copy.53, s32[32]{0:T(128)S(1)} %eq.15), kind=kOutput, calls=%fused_computation.10 | convolution fusion | flops 142607360 | bytes 16777344 | tf_op jit(solution)/shard_map/jb,jrc->brc/dot_general | solution.py:75
  237.4 1.1 copy-done.1
  238.5 2.8 add_convert_fusion
  241.3 6.5 %copy.55 = bf16[32,128,512]{2,1,0:T(8,128)(2,1)} copy(bf16[32,128,512]{2,0,1:T(8,128)(2,1)} %add_convert_fusion) | data formatting | bytes 8388608 | tf_op jit(solution)/shard_map/convert_element_type | solution.py:82
  247.8 82.2 %reduce-scatter.3.cloned.1.call-done = bf16[256,512]{1,0:T(8,128)(2,1)} async-done(((bf16[4096,512]{1,0:T(8,128)(2,1)}), bf16[256,512]{1,0:T(8,128)(2,1)}) %reduce-scatter.3.cloned.1.call-update) | async-done | bytes 262160 | tf_op jit(solution)/shard_map/reduce_scatter | solution.py:81
  330.0 7.9 %fusion.2 = bf16[8192,512]{0,1:T(8,128)(2,1)} fusion(bf16[256,512]{1,0:T(8,128)(2,1)} %reduce-scatter.3.cloned.1.call-done, bf16[256,8192]{1,0:T(8,128)(2,1)} %all-gather.4.cloned.1.call-done), kind=kOutput, calls=%fused_computation.5 | convolution fusion | flops 2151677952 | bytes 12845056 | tf_op jit(solution)/shard_map/rf,rc->fc/dot_general | solution.py:88
  337.9 14.7 %fusion.29 = bf16[16,64,2,128]{3,1,2,0:T(8,128)(2,1)S(1)} fusion(bf16[16,256,2,128]{3,2,1,0:T(2,128)(2,1)S(1)} %reshape.78, f32[16,2,256,64]{2,3,1,0:T(8,128)} %fusion.19, f32[16,2,64,256]{3,2,1,0:T(8,128)} %get-tuple-element.19, f32[16,2,64]{2,1,0:T(2,128)S(1)} %get-tuple-element.18), kind=kOutput, calls=%fused_computation.34 | convolution fusion | flops 138152192 | bytes 6823936 | tf_op jit(solution)/shard_map/chqk,ckhd->cqhd/dot_general | solution.py:54
  353.2 6.6 %fusion.32 = bf16[16,64,2,128]{3,1,2,0:T(8,128)(2,1)S(1)} fusion(bf16[16,256,2,128]{3,2,1,0:T(2,128)(2,1)} %reshape.77, f32[16,2,64]{2,1,0:T(2,128)S(1)} %get-tuple-element.18, f32[16,2,256,64]{2,3,1,0:T(8,128)} %copy-done.3), kind=kOutput, calls=%fused_computation.35 | convolution fusion | flops 137103616 | bytes 4726784 | tf_op jit(solution)/shard_map/chqk,ckhd->cqhd/dot_general | solution.py:46
  360.3 1.1 copy_bitcast_fusion
  361.4 66.7 %reduce-scatter.5.cloned.1.call-done = bf16[512,512]{0,1:T(8,128)(2,1)} async-done(((bf16[8192,512]{0,1:T(8,128)(2,1)}), bf16[512,512]{0,1:T(8,128)(2,1)}) %reduce-scatter.5.cloned.1.call-update) | async-done | bytes 524304 | tf_op jit(solution)/shard_map/reduce_scatter | solution.py:87
  428.1 1.1 fusion.63
  429.3 1.0 copy.57
  430.3 1.0 copy.56
  (34 shorter events, 5.0 us)
Async XLA Ops:
  7.2 47.8 %all-gather.4.cloned.1.call-start = ((), (), s32[]{:S(2)}) async-start(), calls=%async_computation.2 | async-start | bytes 4456448 | tf_op jit(solution)/shard_map/all_gather | solution.py:23
  7.9 100.8 %all-gather.8.cloned.1.call-start = ((), (), s32[]{:S(2)}) async-start(), calls=%async_computation.4 | async-start | bytes 2228224 | tf_op jit(solution)/shard_map/all_gather | solution.py:31
  60.4 5.8 %copy-start.6 = (s32[16,2]{0,1:T(2,128)S(1)}, s32[16,2]{0,1:T(2,128)}, u32[]{:S(2)}) copy-start(s32[16,2]{0,1:T(2,128)} %param.10) | copy-start | bytes 388
  60.4 6.1 %copy-start.4 = (bf16[1024,256]{1,0:T(8,128)(2,1)S(1)}, bf16[1024,256]{1,0:T(8,128)(2,1)}, u32[]{:S(2)}) copy-start(bf16[1024,256]{1,0:T(8,128)(2,1)} %param.6) | copy-start | bytes 1572868
  60.4 6.3 %copy-start.5 = (bf16[1024,256]{1,0:T(8,128)(2,1)S(1)}, bf16[1024,256]{1,0:T(8,128)(2,1)}, u32[]{:S(2)}) copy-start(bf16[1024,256]{1,0:T(8,128)(2,1)} %param.11) | copy-start | bytes 1572868
  60.4 100.7 %all-gather.6.cloned.1.call-start = ((), (), s32[]{:S(2)}) async-start(), calls=%async_computation.3 | async-start | bytes 2228224 | tf_op jit(solution)/shard_map/all_gather | solution.py:32
  65.9 264.1 %reduce-scatter.3.cloned.1.call-start = ((), (), s32[]{:S(2)}) async-start(), calls=%async_computation.5 | async-start | bytes 4456448 | tf_op jit(solution)/shard_map/reduce_scatter | solution.py:81
  169.5 2.1 copy-start.3
  169.5 3.1 copy-start.2
  232.5 4.8 %copy-start = (f32[32,128,256]{2,0,1:T(8,128)S(1)}, f32[32,128,256]{2,0,1:T(8,128)}, u32[]{:S(2)}) copy-start(f32[32,128,256]{2,0,1:T(8,128)} %copy.53) | copy-start | bytes 12582916
  232.5 5.9 %copy-start.1 = (f32[32,128,256]{2,0,1:T(8,128)S(1)}, f32[32,128,256]{2,0,1:T(8,128)}, u32[]{:S(2)}) copy-start(f32[32,128,256]{2,0,1:T(8,128)} %copy.54) | copy-start | bytes 12582916
  247.8 180.4 %reduce-scatter.5.cloned.1.call-start = ((), (), s32[]{:S(2)}) async-start(), calls=%async_computation.6 | async-start | bytes 8912896 | tf_op jit(solution)/shard_map/reduce_scatter | solution.py:87
Sparse Core Ops, SparseCore 0:
  9.8 45.0 all-gather.3
  60.5 48.1 all-gather.7
  111.7 49.3 all-gather.5
  247.9 82.0 reduce-scatter.2
  338.0 90.0 reduce-scatter.4
where the time goes:
time: 439 us; the launch traced here: 438 us
  waiting for transfers between devices  285 us (65%)
  matrix products  76.7 us (17%)
  local copies, waits for them, and re-layouts  60.1 us (14%)
  between operations  13.9 us (3%)
    reduce_scatter x1, waiting for transfers between devices, local(): lax.psum_scatter(summed_rows.reshape(own_rows * lax.axis_size('seq'), 2 *...  82.2 us
    reduce_scatter x1, waiting for transfers between devices, local(): lax.psum_scatter(jnp.einsum('rf,rc->fc', full_states, own_grad, preferred...  66.7 us
    all_gather x1, waiting for transfers between devices, local(): full_states = lax.all_gather(states, 'head', axis=1, tiled=True)  47 us
    all_gather x1, waiting for transfers between devices, local(): lax.all_gather(own_values, 'seq', axis=0, tiled=True)  46.3 us
    all_gather x1, waiting for transfers between devices, local(): lax.all_gather(own_keys, 'seq', axis=0, tiled=True)  41.9 us
    dot_general x1, matrix products, local(): jnp.einsum('chqk,cqhd->ckhd', score_grad, queries_here, preferred_element...  17.6 us
    dot_general x1, matrix products, local(): jnp.einsum('chqk,ckhd->cqhd', score_grad, key_rows, preferred_element_typ...  14.7 us
    reshape x2, local copies, waits for them, and re-layouts, local(): key_part.reshape(span_count * TOPN, NBR, head_cols)  10.3 us
  transfers between devices with their start and end apart: 5, of which 5 were waited for; matrix products, arithmetic and copies ran while one was open for 8% of the time, Pallas kernels for 0%

commit v1 on v0

v1 whole, which is shorter than its diff:
```python
import math

import jax
import jax.numpy as jnp
from jax import lax
from jax.experimental import pallas as pl
from jax.experimental.pallas import tpu as pltpu
from jax.sharding import PartitionSpec as P

HD = 128
SPAN = 64
NBR = 128
TOPN = 2
SCALE = 1.0 / math.sqrt(HD)
MIB = 1 << 20


def dot_nt(a, b):
    return lax.dot_general(a, b, (((1,), (1,)), ((), ())), preferred_element_type=jnp.float32)


def dot_tn(a, b):
    return lax.dot_general(a, b, (((0,), (0,)), ((), ())), preferred_element_type=jnp.float32)


def dot_nn(a, b):
    return jnp.dot(a, b, preferred_element_type=jnp.float32)


def attend_kernel(ids_ref, q_ref, g_ref, kv_ref, ctx_ref, dq_ref, dkv_ref, acc_ref):
    cols = q_ref.shape[1]
    spans = q_ref.shape[0] // SPAN
    pool = kv_ref.shape[0]
    first = lax.broadcasted_iota(jnp.int32, (SPAN, cols), 1) < HD

    def clear(i, _):
        acc_ref[pl.ds(i * NBR, NBR), :] = jnp.zeros((NBR, 2 * cols), jnp.float32)
        return 0

    lax.fori_loop(0, pool // NBR, clear, 0)

    def stack(x):
        zero = jnp.zeros_like(x)
        return jnp.concatenate([jnp.where(first, x, zero), jnp.where(first, zero, x)], axis=0)

    def unstack(x):
        return jnp.where(first, x[:SPAN], x[SPAN:])

    def span(c, _):
        rows = pl.ds(c * SPAN, SPAN)
        at0 = pl.ds(ids_ref[c, 0] * NBR, NBR)
        at1 = pl.ds(ids_ref[c, 1] * NBR, NBR)
        keys = jnp.concatenate([kv_ref[at0, :cols], kv_ref[at1, :cols]], axis=0)
        values = jnp.concatenate([kv_ref[at0, cols:], kv_ref[at1, cols:]], axis=0)
        q2 = stack(q_ref[rows, :])
        g2 = stack(g_ref[rows, :])
        scores = dot_nt(q2, keys) * SCALE
        prob_grad = dot_nt(g2, values)
        top = jnp.max(scores, axis=-1, keepdims=True)
        e = jnp.exp(scores - top)
        probs = e / jnp.sum(e, axis=-1, keepdims=True)
        low = probs.astype(jnp.bfloat16)
        delta = jnp.sum(probs * prob_grad, axis=-1, keepdims=True)
        sg = (probs * (prob_grad - delta) * SCALE).astype(jnp.bfloat16)
        ctx_ref[rows, :] = unstack(dot_nn(low, values)).astype(jnp.bfloat16)
        dq_ref[rows, :] = unstack(dot_nn(sg, keys)).astype(jnp.bfloat16)
        dk = dot_tn(sg, q2)
        dv = dot_tn(low, g2)
        acc_ref[at0, :cols] += dk[:NBR]
        acc_ref[at0, cols:] += dv[:NBR]
        acc_ref[at1, :cols] += dk[NBR:]
        acc_ref[at1, cols:] += dv[NBR:]
        return 0

    lax.fori_loop(0, spans, span, 0)

    def store(i, _):
        at = pl.ds(i * NBR, NBR)
        dkv_ref[at, :] = acc_ref[at, :].astype(jnp.bfloat16)
        return 0

    lax.fori_loop(0, pool // NBR, store, 0)


def attend(ids, queries, grads, kv):
    rows, cols = queries.shape
    pool = kv.shape[0]
    vmem = pl.BlockSpec(memory_space=pltpu.VMEM)
    return pl.pallas_call(
        attend_kernel,
        out_shape=(
            jax.ShapeDtypeStruct((rows, cols), jnp.bfloat16),
            jax.ShapeDtypeStruct((rows, cols), jnp.bfloat16),
            jax.ShapeDtypeStruct((pool, 2 * cols), jnp.bfloat16),
        ),
        in_specs=[pl.BlockSpec(memory_space=pltpu.SMEM), vmem, vmem, vmem],
        out_specs=(vmem, vmem, vmem),
        scratch_shapes=[pltpu.VMEM((pool, 2 * cols), jnp.float32)],
        compiler_params=pltpu.CompilerParams(vmem_limit_bytes=40 * MIB),
        name="attend",
    )(ids, queries, grads, kv)


def local(queries, states, key_weight, value_weight, neighbour_ids, out_grad):
    cols = queries.shape[1]
    full_states = lax.all_gather(states, "head", axis=1, tiled=True)
    keys = dot_nn(full_states, key_weight).astype(jnp.bfloat16)
    values = dot_nn(full_states, value_weight).astype(jnp.bfloat16)
    own = jnp.concatenate([keys, values], axis=1)
    kv = lax.all_gather(own, "seq", axis=0, tiled=True)
    context, query_grad, dkv = attend(neighbour_ids, queries, out_grad, kv)
    own_grad = lax.psum_scatter(dkv, "seq", scatter_dimension=0, tiled=True)
    grads = lax.psum_scatter(
        dot_tn(full_states, own_grad).astype(jnp.bfloat16), "seq", scatter_dimension=0, tiled=True
    ).astype(jnp.float32)
    return context, query_grad, grads[:, :cols], grads[:, cols:]


def solution(mesh):
    in_specs = (
        P("seq", "head"),
        P("seq", "head"),
        P(None, "head"),
        P(None, "head"),
        P("seq", None),
        P("seq", "head"),
    )
    out_specs = (P("seq", "head"), P("seq", "head"), P("seq", "head"), P("seq", "head"))
    return jax.shard_map(local, mesh=mesh, in_specs=in_specs, out_specs=out_specs, check_vma=False)
```

time: 439 us -> 326 us (0.74)
  matrix products: 76.7 us -> 14 us
  local copies, waits for them, and re-layouts: 60.1 us -> 8.44 us
  Pallas kernels: 0 us -> 14 us
  waiting for transfers between devices: 285 us -> 275 us
    dot_general x11 -> x3, matrix products: 76.7 us -> 14 us  [the longest x1 7.87 us: dot_tn(): lax.dot_general(a, b, (((0,), (0,)), ((), ())), preferred_element_type=jn...]
    all_gather x2 -> x1, waiting for transfers between devices: 88.2 us -> 55.1 us  [local(): kv = lax.all_gather(own, 'seq', axis=0, tiled=True)]
    reshape x9 -> x0, local copies, waits for them, and re-layouts: 28.5 us -> none  [the longest x2 10.3 us: local(): key_part.reshape(span_count * TOPN, NBR, head_cols)]
    reduce_scatter x2, waiting for transfers between devices: 149 us -> 172 us  [the longest x1 89.7 us: local(): lax.psum_scatter(dot_tn(full_states, own_grad).astype(jnp.bfloat16), 'seq...]
    pallas_call x0 -> x1, Pallas kernels: none -> 14 us  [attend(): pl.pallas_call(attend_kernel, out_shape=(jax.ShapeDtypeStruct((rows, cols...]
    transpose x2 -> x0, local copies, waits for them, and re-layouts: 11 us -> none  [the longest x1 5.5 us: local(): jnp.einsum('chqk,cqhd->ckhd', score_grad, queries_here, preferred_element...]
    convert_element_type x3 -> x0, local copies, waits for them, and re-layouts: 7.56 us -> none  [the longest x1 6.46 us: local(): summed_rows.reshape(own_rows * lax.axis_size('seq'), 2 * head_cols)]
    gather x2 -> x0, local copies, waits for them, and re-layouts: 7.2 us -> none  [the longest x1 3.61 us: local(): value_rows = pool_values.reshape(block_count, NBR, head_cols)[neighbour_ids]]
  transfers between devices with their start and end apart: 5 -> 4, of which waited for: 5 -> 4; matrix products, arithmetic and copies ran while one was open for 8% -> 0% of each run, Pallas kernels for 0% -> 0%
where the time goes in v1:
time: 326 us
  waiting for transfers between devices  275 us (84%)
  matrix products  14 us (4%)
  Pallas kernels  14 us (4%)
  between operations  13.8 us (4%)
  local copies, waits for them, and re-layouts  8.44 us (3%)
    reduce_scatter x1, waiting for transfers between devices, local(): lax.psum_scatter(dot_tn(full_states, own_grad).astype(jnp.bfloat16), 'seq...  89.7 us
    reduce_scatter x1, waiting for transfers between devices, local(): own_grad = lax.psum_scatter(dkv, 'seq', scatter_dimension=0, tiled=True)  82.2 us
    all_gather x1, waiting for transfers between devices, local(): kv = lax.all_gather(own, 'seq', axis=0, tiled=True)  55.1 us
    all_gather x1, waiting for transfers between devices, local(): full_states = lax.all_gather(states, 'head', axis=1, tiled=True)  47 us
    pallas_call x1, Pallas kernels, attend(): pl.pallas_call(attend_kernel, out_shape=(jax.ShapeDtypeStruct((rows, cols...  14 us
    dot_general x1, matrix products, dot_tn(): lax.dot_general(a, b, (((0,), (0,)), ((), ())), preferred_element_type=jn...  7.87 us
    unnamed x17, local copies, waits for them, and re-layouts  7.29 us
  transfers between devices with their start and end apart: 4, of which 4 were waited for; matrix products, arithmetic and copies ran while one was open for 0% of the time, Pallas kernels for 0%

profile of v1, /device:TPU:2, one launch (start us, length us, event | category | flops | bytes accessed | tf_op | source)
XLA Modules:
  0.0 325.8 jit_solution(9847576444515660770)
XLA Ops:
  7.2 0.0 all-gather.3.cloned.1.call-start
  7.2 0.7 all-gather.3.cloned.1.call-update
  7.9 0.0 all-gather.5.cloned.1.call-start
  7.9 47.0 %all-gather.3.cloned.1.call-done = bf16[256,8192]{1,0:T(8,128)(2,1)} async-done(((bf16[256,512]{1,0:T(8,128)(2,1)}), bf16[256,8192]{1,0:T(8,128)(2,1)}) %all-gather.3.cloned.1.call-update) | async-done | bytes 4194320 | tf_op jit(solution)/shard_map/all_gather | solution.py:106
  55.0 0.0 copy-start.4
  55.0 0.0 copy-start.6
  55.0 4.8 %convolution_convert_fusion.1 = bf16[256,256]{1,0:T(8,128)(2,1)S(1)} fusion(bf16[256,8192]{1,0:T(8,128)(2,1)} %all-gather.3.cloned.1.call-done, bf16[8192,256]{1,0:T(8,128)(2,1)} %param.9), kind=kOutput, calls=%fused_computation.2 | convolution fusion | flops 1073807360 | bytes 8519680 | tf_op jit(solution)/shard_map/dot_general | solution.py:27
  59.8 0.0 copy-done.4
  59.8 1.1 copy-done.6
  60.9 0.0 copy-start.5
  60.9 0.0 copy-start.2
  60.9 1.2 convolution_convert_fusion.2
  62.1 0.7 pad_maximum_fusion
  62.9 0.0 all-gather.5.cloned.1.call-update
  62.9 0.0 reduce-scatter.3.cloned.1.call-start
  62.9 0.0 copy-done.5
  62.9 0.1 copy.12.ids_ref
  63.0 55.1 %all-gather.5.cloned.1.call-done.kv_ref = bf16[4096,512]{1,0:T(8,128)(2,1)} async-done(((bf16[256,512]{1,0:T(8,128)(2,1)}), bf16[4096,512]{1,0:T(8,128)(2,1)}) %all-gather.5.cloned.1.call-update) | async-done | bytes 4194320 | tf_op jit(solution)/shard_map/all_gather | solution.py:110
  118.2 0.0 copy-done.2
  118.2 0.0 copy-done.3
  118.2 2.2 copy-done
  120.4 14.0 %attend.1 = (bf16[1024,256]{1,0:T(8,128)(2,1)}, bf16[1024,256]{1,0:T(8,128)(2,1)}, bf16[4096,512]{1,0:T(8,128)(2,1)S(1)}) custom-call(s32[16,2]{1,0:T(8,128)S(1)} %copy.12.ids_ref, bf16[1024,256]{1,0:T(8,128)(2,1)S(1)} %copy-done.2, bf16[1024,256]{1,0:T(8,128)(2,1)S(1)} %copy-done.3, bf16[4096,512]{1,0:T(8,128)(2,1)S(1)} %copy-done), custom_call_target="tpu_custom_call" | custom-call | tf_op jit(solution)/shard_map/attend/pallas_call | solution.py:89
  134.3 2.0 copy-done.1
  136.3 0.0 reduce-scatter.3.cloned.1.call-update
  136.3 0.0 reduce-scatter.5.cloned.1.call-start
  136.4 82.2 %reduce-scatter.3.cloned.1.call-done = bf16[256,512]{1,0:T(8,128)(2,1)} async-done(((bf16[4096,512]{1,0:T(8,128)(2,1)}), bf16[256,512]{1,0:T(8,128)(2,1)}) %reduce-scatter.3.cloned.1.call-update) | async-done | bytes 262160 | tf_op jit(solution)/shard_map/reduce_scatter | solution.py:112
  218.5 7.9 %fusion = bf16[8192,512]{0,1:T(8,128)(2,1)} fusion(bf16[256,512]{1,0:T(8,128)(2,1)} %reduce-scatter.3.cloned.1.call-done, bf16[256,8192]{1,0:T(8,128)(2,1)} %all-gather.3.cloned.1.call-done), kind=kOutput, calls=%fused_computation.1 | convolution fusion | flops 2151677952 | bytes 12845056 | tf_op jit(solution)/shard_map/dot_general | solution.py:23
  226.4 0.0 reduce-scatter.5.cloned.1.call-update
  226.4 89.7 %reduce-scatter.5.cloned.1.call-done = bf16[512,512]{0,1:T(8,128)(2,1)} async-done(((bf16[8192,512]{0,1:T(8,128)(2,1)}), bf16[512,512]{0,1:T(8,128)(2,1)}) %reduce-scatter.5.cloned.1.call-update) | async-done | bytes 524304 | tf_op jit(solution)/shard_map/reduce_scatter | solution.py:113
  316.1 1.1 fusion.1
  317.3 1.0 copy.14
  318.3 1.0 copy.13
  (3 shorter events, 0.0 us)
Async XLA Ops:
  7.2 47.8 %all-gather.3.cloned.1.call-start = ((), (), s32[]{:S(2)}) async-start(), calls=%async_computation.2 | async-start | bytes 4456448 | tf_op jit(solution)/shard_map/all_gather | solution.py:106
  7.9 110.3 %all-gather.5.cloned.1.call-start = ((), (), s32[]{:S(2)}) async-start(), calls=%async_computation.3 | async-start | bytes 4456448 | tf_op jit(solution)/shard_map/all_gather | solution.py:110
  55.0 4.9 %copy-start.4 = (bf16[256,8192]{1,0:T(8,128)(2,1)S(1)}, bf16[256,8192]{1,0:T(8,128)(2,1)}, u32[]{:S(2)}) copy-start(bf16[256,8192]{1,0:T(8,128)(2,1)} %all-gather.3.cloned.1.call-done) | copy-start | bytes 12582916
  55.0 5.9 %copy-start.6 = (bf16[8192,256]{1,0:T(8,128)(2,1)S(1)}, bf16[8192,256]{1,0:T(8,128)(2,1)}, u32[]{:S(2)}) copy-start(bf16[8192,256]{1,0:T(8,128)(2,1)} %param.8) | copy-start | bytes 12582916
  60.9 2.1 copy-start.5
  60.9 57.3 %copy-start.2 = (bf16[1024,256]{1,0:T(8,128)(2,1)S(1)}, bf16[1024,256]{1,0:T(8,128)(2,1)}, u32[]{:S(2)}) copy-start(bf16[1024,256]{1,0:T(8,128)(2,1)} %q_ref.1) | copy-start | bytes 1572868
  60.9 57.3 %copy-start.3 = (bf16[1024,256]{1,0:T(8,128)(2,1)S(1)}, bf16[1024,256]{1,0:T(8,128)(2,1)}, u32[]{:S(2)}) copy-start(bf16[1024,256]{1,0:T(8,128)(2,1)} %g_ref.1) | copy-start | bytes 1572868
  62.9 155.6 %reduce-scatter.3.cloned.1.call-start = ((), (), s32[]{:S(2)}) async-start(), calls=%async_computation.4 | async-start | bytes 4456448 | tf_op jit(solution)/shard_map/reduce_scatter | solution.py:112
  118.2 2.2 copy-start
  134.3 2.0 copy-start.1
  136.3 179.8 %reduce-scatter.5.cloned.1.call-start = ((), (), s32[]{:S(2)}) async-start(), calls=%async_computation.5 | async-start | bytes 8912896 | tf_op jit(solution)/shard_map/reduce_scatter | solution.py:113
Sparse Core Ops, SparseCore 0:
  9.8 45.0 all-gather.2
  63.0 55.1 all-gather.4
  136.4 82.0 reduce-scatter.2
  226.5 89.5 reduce-scatter.4

commit v2 on v1

v2 whole, which is shorter than its diff:
```python
import math

import jax
import jax.numpy as jnp
from jax import lax
from jax.experimental import pallas as pl
from jax.experimental.pallas import tpu as pltpu
from jax.sharding import PartitionSpec as P

HD = 128
SPAN = 64
NBR = 128
TOPN = 2
SCALE = 1.0 / math.sqrt(HD)
MIB = 1 << 20
MESH = pl.DeviceIdType.MESH
SIDE = 4
RING = 8


def dot_nt(a, b):
    return lax.dot_general(a, b, (((1,), (1,)), ((), ())), preferred_element_type=jnp.float32)


def dot_tn(a, b):
    return lax.dot_general(a, b, (((0,), (0,)), ((), ())), preferred_element_type=jnp.float32)


def dot_nn(a, b):
    return jnp.dot(a, b, preferred_element_type=jnp.float32)


def attend_kernel(ids_ref, q_ref, g_ref, kv_ref, ctx_ref, dq_ref, dkv_ref, acc_ref):
    cols = q_ref.shape[1]
    spans = q_ref.shape[0] // SPAN
    blocks = kv_ref.shape[1]
    first = lax.broadcasted_iota(jnp.int32, (SPAN, cols), 1) < HD

    def clear(i, _):
        for j in range(2):
            acc_ref[j, i] = jnp.zeros((NBR, cols), jnp.float32)
        return 0

    lax.fori_loop(0, blocks, clear, 0)

    def stack(x):
        zero = jnp.zeros_like(x)
        return jnp.concatenate([jnp.where(first, x, zero), jnp.where(first, zero, x)], axis=0)

    def unstack(x):
        return jnp.where(first, x[:SPAN], x[SPAN:])

    def span(c, _):
        rows = pl.ds(c * SPAN, SPAN)
        id0, id1 = ids_ref[c, 0], ids_ref[c, 1]
        keys = jnp.concatenate([kv_ref[0, id0], kv_ref[0, id1]], axis=0)
        values = jnp.concatenate([kv_ref[1, id0], kv_ref[1, id1]], axis=0)
        q2 = stack(q_ref[rows, :])
        g2 = stack(g_ref[rows, :])
        scores = dot_nt(q2, keys) * SCALE
        prob_grad = dot_nt(g2, values)
        top = jnp.max(scores, axis=-1, keepdims=True)
        e = jnp.exp(scores - top)
        probs = e / jnp.sum(e, axis=-1, keepdims=True)
        low = probs.astype(jnp.bfloat16)
        delta = jnp.sum(probs * prob_grad, axis=-1, keepdims=True)
        sg = (probs * (prob_grad - delta) * SCALE).astype(jnp.bfloat16)
        ctx_ref[rows, :] = unstack(dot_nn(low, values)).astype(jnp.bfloat16)
        dq_ref[rows, :] = unstack(dot_nn(sg, keys)).astype(jnp.bfloat16)
        dk = dot_tn(sg, q2)
        dv = dot_tn(low, g2)
        acc_ref[0, id0] += dk[:NBR]
        acc_ref[1, id0] += dv[:NBR]
        acc_ref[0, id1] += dk[NBR:]
        acc_ref[1, id1] += dv[NBR:]
        return 0

    lax.fori_loop(0, spans, span, 0)

    def store(i, _):
        for j in range(2):
            dkv_ref[j, i] = acc_ref[j, i].astype(jnp.bfloat16)
        return 0

    lax.fori_loop(0, blocks, store, 0)


def attend(ids, queries, grads, kv):
    rows, cols = queries.shape
    blocks = kv.shape[1] * kv.shape[2] // NBR
    vmem = pl.BlockSpec(memory_space=pltpu.VMEM)
    context, query_grad, dkv = pl.pallas_call(
        attend_kernel,
        out_shape=(
            jax.ShapeDtypeStruct((rows, cols), jnp.bfloat16),
            jax.ShapeDtypeStruct((rows, cols), jnp.bfloat16),
            jax.ShapeDtypeStruct((2, blocks, NBR, cols), jnp.bfloat16),
        ),
        in_specs=[pl.BlockSpec(memory_space=pltpu.SMEM), vmem, vmem, vmem],
        out_specs=(vmem, vmem, vmem),
        scratch_shapes=[pltpu.VMEM((2, blocks, NBR, cols), jnp.float32)],
        compiler_params=pltpu.CompilerParams(vmem_limit_bytes=40 * MIB),
        name="attend",
    )(ids, queries, grads, kv.reshape(2, blocks, NBR, cols))
    return context, query_grad, dkv.reshape(kv.shape)


def wrap(i, n):
    return lax.rem(i + n, n)


class Place:
    def __init__(self):
        self.seq = lax.axis_index("seq")
        self.head = lax.axis_index("head")
        self.x, self.y = self.seq // SIDE, lax.rem(self.seq, SIDE)
        self.z, self.core = self.head // 2, lax.rem(self.head, 2)

    def along(self, is_x, step):
        if is_x:
            return (wrap(self.x + step, SIDE) * SIDE + self.y, self.head)
        return (self.x * SIDE + wrap(self.y + step, SIDE), self.head)

    def ring(self, step):
        return (self.seq, wrap(self.z + step, RING) * 2 + self.core)

    def twin(self):
        return (self.seq, self.z * 2 + 1 - self.core)

    def slot(self, first_is_x, first, second):
        if first_is_x:
            return wrap(self.x + first, SIDE) * SIDE + wrap(self.y + second, SIDE)
        return wrap(self.x + second, SIDE) * SIDE + wrap(self.y + first, SIDE)


def greet(devices):
    barrier = pltpu.get_barrier_semaphore()
    for device in devices:
        pl.semaphore_signal(barrier, inc=1, device_id=device, device_id_type=MESH)
    pl.semaphore_wait(barrier, len(devices))


class Sender:
    def __init__(self, sems):
        self.sems, self.started = sems, []

    def send(self, src, dst, recv_sem, device):
        copy = pltpu.make_async_remote_copy(
            src_ref=src,
            dst_ref=dst,
            send_sem=self.sems.at[len(self.started)],
            recv_sem=recv_sem,
            device_id=device,
            device_id_type=MESH,
        )
        copy.start()
        self.started.append(copy)

    def finish(self):
        for copy in self.started:
            copy.wait_send()


def arrived(ref, send_sem, recv_sem, device):
    pltpu.make_async_remote_copy(
        src_ref=ref, dst_ref=ref, send_sem=send_sem, recv_sem=recv_sem, device_id=device, device_id_type=MESH
    ).wait_recv()


class Gather:
    def __init__(self, place, sender, buf, recv, j, first_is_x, cid, row, rows, sign):
        self.place, self.sender, self.buf, self.recv = place, sender, buf, recv
        self.j, self.fx, self.cid, self.row, self.rows, self.sign = j, first_is_x, cid, row, rows, sign

    def ref(self, slot):
        return self.buf.at[self.j, slot, pl.ds(self.row, self.rows), :]

    def send(self, offsets, is_x, step):
        slot = self.place.slot(self.fx, *offsets)
        self.sender.send(
            self.ref(slot), self.ref(slot), self.recv.at[self.j, slot, self.cid], self.place.along(is_x, step)
        )

    def wait(self, offsets):
        slot = self.place.slot(self.fx, *offsets)
        arrived(self.ref(slot), self.sender.sems.at[0], self.recv.at[self.j, slot, self.cid], self.place.twin())

    def spread(self, first):
        self.send((first, 0), not self.fx, self.sign)
        self.send((first, 0), not self.fx, -self.sign)

    def begin(self):
        self.send((0, 0), self.fx, self.sign)
        self.send((0, 0), self.fx, -self.sign)
        self.spread(0)

    def near(self):
        self.wait((-self.sign, 0))
        self.send((-self.sign, 0), self.fx, self.sign)
        self.spread(-self.sign)
        self.wait((self.sign, 0))
        self.spread(self.sign)

    def far(self):
        self.wait((-2 * self.sign, 0))
        self.spread(2)

    def relay(self, first):
        self.wait((first, -self.sign))
        self.send((first, -self.sign), not self.fx, self.sign)

    def relays(self):
        return [0, -self.sign, self.sign, 2]

    def end(self):
        for first in self.relays():
            self.wait((first, self.sign))
            self.wait((first, 2))


def pool_kernel(states_ref, kw_ref, vw_ref, kv_ref, part_ref, st, w, acc, send_sems, twin_recv, ring_recv, pool_recv, w_sems):
    place = Place()
    heads, rows, feats = st.shape
    cols = kv_ref.shape[3]
    half = rows // 2
    loads = [pltpu.make_async_copy(kw_ref, w.at[0], w_sems.at[0]), pltpu.make_async_copy(vw_ref, w.at[1], w_sems.at[1])]
    for load in loads:
        load.start()
    st[place.head] = states_ref[...]
    acc[...] = jnp.zeros_like(acc)
    greet([place.ring(1), place.ring(-1), place.twin()] + [place.along(i, d) for i in (True, False) for d in (1, -1)])
    sender = Sender(send_sems)

    def ref(slot, g):
        return st.at[slot, pl.ds(g * half, half), :]

    def slot_at(distance, other):
        core = 1 - place.core if other else place.core
        return wrap(place.z + distance, RING) * 2 + core

    def to_ring(slot, g, sign):
        sender.send(ref(slot, g), ref(slot, g), ring_recv.at[slot, g], place.ring(sign))

    def to_twin(slot, g):
        sender.send(ref(slot, g), ref(slot, g), twin_recv.at[slot, g], place.twin())

    def multiply(slot, g):
        at = pl.ds(g * half, half)
        left = st[slot, at, :]
        acc[at, :cols] += dot_nn(left, w[0, slot])
        acc[at, cols:] += dot_nn(left, w[1, slot])

    def signs(d, g):
        return (1, -1) if d < RING // 2 else ((1,) if g == 0 else (-1,))

    def hop(g, d):
        for sign in signs(d, g):
            slot = slot_at(-sign * d, False)
            arrived(ref(slot, g), send_sems.at[0], ring_recv.at[slot, g], place.twin())
            if sign in signs(d + 1, g) and d < RING // 2:
                to_ring(slot, g, sign)
            to_twin(slot, g)

    def own(g, d):
        for sign in signs(d, g) if d else (1,):
            multiply(slot_at(-sign * d, False), g)

    def other(g, d):
        for sign in signs(d, g) if d else (1,):
            slot = slot_at(-sign * d, True)
            arrived(ref(slot, g), send_sems.at[0], twin_recv.at[slot, g], place.twin())
            multiply(slot, g)

    def project(g):
        at = pl.ds(g * half, half)
        kv_ref[0, place.seq, at, :] = acc[at, :cols].astype(kv_ref.dtype)
        kv_ref[1, place.seq, at, :] = acc[at, cols:].astype(kv_ref.dtype)

    def gathers(g):
        quarter = half // 2
        return [
            Gather(place, sender, kv_ref, pool_recv, j, j == 0, 2 * g + i, g * half + i * quarter, quarter, sign)
            for i, sign in enumerate((1, -1))
            for j in range(2)
        ]

    for g in range(2):
        for sign in (1, -1):
            to_ring(place.head, g, sign)
        to_twin(place.head, g)
    for load in loads:
        load.wait()
    hop(0, 1)
    own(0, 0)
    hop(1, 1)
    hop(0, 2)
    other(0, 0)
    own(0, 1)
    hop(1, 2)
    hop(0, 3)
    other(0, 1)
    own(0, 2)
    hop(1, 3)
    hop(0, 4)
    other(0, 2)
    own(0, 3)
    other(0, 3)
    own(0, 4)
    other(0, 4)
    project(0)
    early = gathers(0)
    for one in early:
        one.begin()
    own(1, 0)
    other(1, 0)
    own(1, 1)
    for one in early:
        one.near()
    hop(1, 4)
    other(1, 1)
    own(1, 2)
    other(1, 2)
    for one in early:
        one.far()
    own(1, 3)
    other(1, 3)
    own(1, 4)
    other(1, 4)
    project(1)
    late = gathers(1)
    for one in late:
        one.begin()
    for i in range(4):
        for one in early:
            one.relay(one.relays()[i])
    for one in late:
        one.near()
    for one in late:
        one.relay(one.relays()[0])
    for one in late:
        one.far()
    mine = pl.ds(pl.multiple_of(place.head * (rows // heads), rows // heads), rows // heads)
    for slot in range(heads):
        part_ref[slot] = st[slot, mine, :]
    for i in range(1, 4):
        for one in late:
            one.relay(one.relays()[i])
    for one in early + late:
        one.end()
    sender.finish()


def pool(states, key_weight, value_weight):
    rows, feats = states.shape
    cols = key_weight.shape[1]
    heads = key_weight.shape[0] // feats
    seqs = SIDE * SIDE
    vmem, anywhere = pl.BlockSpec(memory_space=pltpu.VMEM), pl.BlockSpec(memory_space=pl.ANY)
    dma = pltpu.SemaphoreType.DMA
    return pl.pallas_call(
        pool_kernel,
        out_shape=(
            jax.ShapeDtypeStruct((2, seqs, rows, cols), jnp.bfloat16),
            jax.ShapeDtypeStruct((heads, rows // heads, feats), jnp.bfloat16),
        ),
        in_specs=[vmem, anywhere, anywhere],
        out_specs=(vmem, vmem),
        scratch_shapes=[
            pltpu.VMEM((heads, rows, feats), jnp.bfloat16),
            pltpu.VMEM((2, heads, feats, cols), jnp.bfloat16),
            pltpu.VMEM((rows, 2 * cols), jnp.float32),
            dma((160,)),
            dma((heads, 2)),
            dma((heads, 2)),
            dma((2, seqs, 4)),
            dma((2,)),
        ],
        compiler_params=pltpu.CompilerParams(
            collective_id=1, has_side_effects=True, vmem_limit_bytes=40 * MIB
        ),
        name="pool",
    )(states, key_weight.reshape(heads, feats, cols), value_weight.reshape(heads, feats, cols))


def reduce_kernel(dkv_ref, all_ref, box, mid, box2, send_sems, box_recv, box2_recv, pool_recv):
    place = Place()
    rows = dkv_ref.shape[2]
    half = rows // 2
    halves = (pl.ds(0, half), pl.ds(half, half))
    offsets = (2, 1, 3, 0)
    greet([place.along(i, d) for i in (True, False) for d in (1, -1)])
    sender = Sender(send_sems)
    ways = ((0, 1), (1, -1))

    def add(*terms):
        total = terms[0].astype(jnp.float32)
        for term in terms[1:]:
            total = total + term.astype(jnp.float32)
        return total.astype(jnp.bfloat16)

    def send1(j, way, sign, kind, k, src):
        sender.send(src, box.at[j, way, kind, k], box_recv.at[j, way, kind, k], place.along(j == 0, sign))

    def wait1(j, way, kind, k):
        arrived(box.at[j, way, kind, k], send_sems.at[0], box_recv.at[j, way, kind, k], place.along(j == 0, 1))

    def send2(j, way, sign, kind, src):
        sender.send(src, box2.at[j, way, kind], box2_recv.at[j, way, kind], place.along(j != 0, sign))

    def wait2(j, way, kind):
        arrived(box2.at[j, way, kind], send_sems.at[0], box2_recv.at[j, way, kind], place.along(j != 0, 1))

    for k, second in enumerate(offsets):
        for j in range(2):
            for way, sign in ways:
                send1(j, way, sign, 0, k, dkv_ref.at[j, place.slot(j == 0, 2, second), halves[way], :])
    for k, second in enumerate(offsets):
        for j in range(2):
            for way, sign in ways:
                send1(j, way, sign, 1, k, dkv_ref.at[j, place.slot(j == 0, sign, second), halves[1 - way], :])
    for k, second in enumerate(offsets):
        for j in range(2):
            for way, sign in ways:
                wait1(j, way, 0, k)
                mine = dkv_ref[j, place.slot(j == 0, sign, second), halves[way], :]
                box[j, way, 0, k] = add(box[j, way, 0, k], mine)
                send1(j, way, sign, 2, k, box.at[j, way, 0, k])
    for k, second in enumerate(offsets):
        for j in range(2):
            for way, sign in ways:
                wait1(j, 1 - way, 1, k)
                wait1(j, way, 2, k)
                mine = dkv_ref[j, place.slot(j == 0, 0, second), halves[way], :]
                mid[j, k, halves[way], :] = add(mine, box[j, 1 - way, 1, k], box[j, way, 2, k])
            if k == 0:
                for way, sign in ways:
                    send2(j, way, sign, 0, mid.at[j, 0, halves[way], :])
            if k in (1, 2):
                way, sign = ways[k - 1]
                send2(j, way, sign, 1, mid.at[j, k, halves[1 - way], :])
    for j in range(2):
        for way, sign in ways:
            wait2(j, way, 0)
            box2[j, way, 0] = add(box2[j, way, 0], mid[j, 1 + way, halves[way], :])
            send2(j, way, sign, 2, box2.at[j, way, 0])
    gathers = []
    for way, sign in ways:
        for j in range(2):
            wait2(j, 1 - way, 1)
            wait2(j, way, 2)
            all_ref[j, place.seq, halves[way], :] = add(
                mid[j, 3, halves[way], :], box2[j, 1 - way, 1], box2[j, way, 2]
            )
            one = Gather(place, sender, all_ref, pool_recv, j, j != 0, way, way * half, half, sign)
            one.begin()
            gathers.append(one)
    for one in gathers:
        one.near()
    for one in gathers:
        one.relay(one.relays()[0])
    for one in gathers:
        one.far()
    for i in range(1, 4):
        for one in gathers:
            one.relay(one.relays()[i])
    for one in gathers:
        one.end()
    sender.finish()


def reduce_all(dkv):
    _, seqs, rows, cols = dkv.shape
    half = rows // 2
    vmem = pl.BlockSpec(memory_space=pltpu.VMEM)
    dma = pltpu.SemaphoreType.DMA
    return pl.pallas_call(
        reduce_kernel,
        out_shape=jax.ShapeDtypeStruct(dkv.shape, jnp.bfloat16),
        in_specs=[vmem],
        out_specs=vmem,
        scratch_shapes=[
            pltpu.VMEM((2, 2, 3, SIDE, half, cols), jnp.bfloat16),
            pltpu.VMEM((2, SIDE, rows, cols), jnp.bfloat16),
            pltpu.VMEM((2, 2, 3, half, cols), jnp.bfloat16),
            dma((128,)),
            dma((2, 2, 3, SIDE)),
            dma((2, 2, 3)),
            dma((2, seqs, 2)),
        ],
        compiler_params=pltpu.CompilerParams(
            collective_id=2, has_side_effects=True, vmem_limit_bytes=32 * MIB
        ),
        name="reduce_all",
    )(dkv)


def weight_kernel(t_ref, dkv_ref, dk_ref, dv_ref):
    heads, seqs, rows, feats = t_ref.shape
    dk_ref[...] = jnp.zeros_like(dk_ref)
    dv_ref[...] = jnp.zeros_like(dv_ref)

    def block(s, _):
        left = t_ref[:, pl.ds(s, 1), :, :].reshape(heads * rows, feats)
        dk_ref[...] += dot_tn(left, dkv_ref[0, s])
        dv_ref[...] += dot_tn(left, dkv_ref[1, s])
        return 0

    lax.fori_loop(0, seqs, block, 0)


def weight_grads(t, dkv):
    heads, seqs, rows, feats = t.shape
    cols = dkv.shape[3]
    vmem = pl.BlockSpec(memory_space=pltpu.VMEM)
    return pl.pallas_call(
        weight_kernel,
        out_shape=(jax.ShapeDtypeStruct((feats, cols), jnp.float32),) * 2,
        in_specs=[vmem, vmem],
        out_specs=(vmem, vmem),
        compiler_params=pltpu.CompilerParams(vmem_limit_bytes=24 * MIB),
        name="weight_grads",
    )(t, dkv)


def local(queries, states, key_weight, value_weight, neighbour_ids, out_grad):
    kv, part = pool(states, key_weight, value_weight)
    column = lax.all_to_all(part, "seq", split_axis=0, concat_axis=0, tiled=True)
    t = lax.all_gather(column, "head", axis=0, tiled=False)
    context, query_grad, dkv = attend(neighbour_ids, queries, out_grad, kv)
    dk, dv = weight_grads(t, reduce_all(dkv))
    return context, query_grad, dk, dv


def solution(mesh):
    in_specs = (
        P("seq", "head"),
        P("seq", "head"),
        P(None, "head"),
        P(None, "head"),
        P("seq", None),
        P("seq", "head"),
    )
    out_specs = (P("seq", "head"), P("seq", "head"), P("seq", "head"), P("seq", "head"))
    return jax.shard_map(local, mesh=mesh, in_specs=in_specs, out_specs=out_specs, check_vma=False)
```

time: 326 us -> 172 us (0.53)
  waiting for transfers between devices: 275 us -> 0.02 us
  Pallas kernels: 14 us -> 127 us
  matrix products: 14 us -> 0 us
  blocking collectives: 0 us -> 13.8 us
  local copies, waits for them, and re-layouts: 8.44 us -> 15.9 us
    reduce_scatter x2 -> x0, waiting for transfers between devices: 172 us -> none  [the longest x1 89.7 us: local(): lax.psum_scatter(dot_tn(full_states, own_grad).astype(jnp.bfloat16), 'seq...]
    pallas_call x0 -> x3, Pallas kernels: none -> 113 us  [the longest x1 62.5 us: pool(): pl.pallas_call(pool_kernel, out_shape=(jax.ShapeDtypeStruct((2, seqs, row...]
    all_gather x2 -> x1, waiting for transfers between devices: 102 us -> 0.01 us  [local(): t = lax.all_gather(column, 'head', axis=0, tiled=False)]
    dot_general x3 -> x0, matrix products: 14 us -> none  [the longest x1 7.87 us: dot_tn(): lax.dot_general(a, b, (((0,), (0,)), ((), ())), preferred_element_type=jn...]
    all_to_all x0 -> x1, blocking collectives: none -> 13.8 us  [local(): lax.all_to_all(part, 'seq', split_axis=0, concat_axis=0, tiled=True)]
    unnamed x17 -> x23, local copies, waits for them, and re-layouts: 7.29 us -> 15.9 us
  transfers between devices with their start and end apart: 4 -> 1, of which waited for: 4 -> 0; matrix products, arithmetic and copies ran while one was open for 0% -> 0% of each run, Pallas kernels for 0% -> 34%
where the time goes in v2:
time: 172 us; the launch traced here: 171 us
  Pallas kernels  127 us (74%)
  local copies, waits for them, and re-layouts  15.9 us (9%)
  between operations  14.1 us (8%)
  blocking collectives  13.8 us (8%)
    pallas_call x1, Pallas kernels, pool(): pl.pallas_call(pool_kernel, out_shape=(jax.ShapeDtypeStruct((2, seqs, row...  62.5 us
    pallas_call x1, Pallas kernels, reduce_all(): pl.pallas_call(reduce_kernel, out_shape=jax.ShapeDtypeStruct(dkv.shape, j...  44.4 us
    unnamed x23, local copies, waits for them, and re-layouts  15.9 us
    pallas_call x1, Pallas kernels, attend(): pl.pallas_call(attend_kernel, out_shape=(jax.ShapeDtypeStruct((rows, cols...  13.9 us
    all_to_all x1, blocking collectives, local(): lax.all_to_all(part, 'seq', split_axis=0, concat_axis=0, tiled=True)  13.8 us
    pallas_call x1, Pallas kernels, weight_grads(): pl.pallas_call(weight_kernel, out_shape=(jax.ShapeDtypeStruct((feats, col...  6.22 us
  transfers between devices with their start and end apart: 1, of which 0 were waited for; matrix products, arithmetic and copies ran while one was open for 0% of the time, Pallas kernels for 34%

profile of v2, /device:TPU:2, one launch (start us, length us, event | category | flops | bytes accessed | tf_op | source)
XLA Modules:
  0.0 170.9 jit_solution(18316976850885813108)
XLA Ops:
  7.2 0.0 all-gather.3.cloned.1.call-start
  7.2 0.0 copy-start.4
  7.2 2.2 %copy-done.4 = bf16[8192,256]{1,0:T(8,128)(2,1)S(1)} copy-done((bf16[8192,256]{1,0:T(8,128)(2,1)S(1)}, bf16[8192,256]{1,0:T(8,128)(2,1)}, u32[]{:S(2)}) %copy-start.4) | copy-done | bytes 4194328
  9.4 0.0 copy-start.5
  9.4 2.2 %copy-done.5 = bf16[8192,256]{1,0:T(8,128)(2,1)S(1)} copy-done((bf16[8192,256]{1,0:T(8,128)(2,1)S(1)}, bf16[8192,256]{1,0:T(8,128)(2,1)}, u32[]{:S(2)}) %copy-start.5) | copy-done | bytes 4194328
  11.6 0.0 copy-start.9
  11.6 0.9 copy-done.9
  12.5 0.0 copy-start.10
  12.5 0.0 copy-start.7
  12.5 0.0 copy-start.8
  12.5 62.5 %pool.1 = (bf16[2,16,256,256]{3,2,1,0:T(8,128)(2,1)S(1)}, bf16[16,16,512]{2,1,0:T(8,128)(2,1)S(1)}) custom-call(bf16[256,512]{1,0:T(8,128)(2,1)S(1)} %copy-done.9, bf16[16,512,256]{2,1,0:T(8,128)(2,1)S(1)} %bitcast.6, bf16[16,512,256]{2,1,0:T(8,128)(2,1)S(1)} %bitcast.7), custom_call_target="tpu_custom_call" | custom-call | tf_op jit(solution)/shard_map/pool/pallas_call | solution.py:360
  75.1 0.0 copy-start.2
  75.1 2.0 %copy-done.2 = bf16[2,16,256,256]{3,2,1,0:T(8,128)(2,1)} copy-done((bf16[2,16,256,256]{3,2,1,0:T(8,128)(2,1)}, bf16[2,16,256,256]{3,2,1,0:T(8,128)(2,1)S(1)}, u32[]{:S(2)}) %copy-start.2) | copy-done | bytes 4194328
  77.0 13.8 %all_to_all.5 = bf16[16,16,512]{2,1,0:T(8,128)(2,1)} all-to-all(bf16[16,16,512]{2,1,0:T(8,128)(2,1)S(1)} %get-tuple-element.14), channel_id=1, replica_groups=mesh['seq'=16,'head'=16] {'seq'}, dimensions={0} | all-to-all | bytes 524288 | tf_op jit(solution)/shard_map/all_to_all | solution.py:527
  90.8 0.0 all-gather.3.cloned.1.call-update
  90.9 0.0 copy-done.10
  90.9 0.1 copy.11.ids_ref
  91.0 0.0 copy-done.7
  91.0 0.0 copy-done.8
  91.0 0.0 copy-start.3
  91.0 2.2 %copy-done.3 = bf16[2,16,256,256]{3,2,1,0:T(8,128)(2,1)S(1)} copy-done((bf16[2,16,256,256]{3,2,1,0:T(8,128)(2,1)S(1)}, bf16[2,16,256,256]{3,2,1,0:T(8,128)(2,1)}, u32[]{:S(2)}) %copy-start.3) | copy-done | bytes 4194328
  93.2 13.9 %attend.1 = (bf16[1024,256]{1,0:T(8,128)(2,1)}, bf16[1024,256]{1,0:T(8,128)(2,1)}, bf16[2,32,128,256]{3,2,1,0:T(8,128)(2,1)S(1)}) custom-call(s32[16,2]{1,0:T(8,128)S(1)} %copy.11.ids_ref, bf16[1024,256]{1,0:T(8,128)(2,1)S(1)} %copy-done.7, bf16[1024,256]{1,0:T(8,128)(2,1)S(1)} %copy-done.8, bf16[2,32,128,256]{3,2,1,0:T(8,128)(2,1)S(1)} %bitcast.5), custom_call_target="tpu_custom_call" | custom-call | tf_op jit(solution)/shard_map/attend/pallas_call | solution.py:92
  107.1 44.4 %reduce_all.1.dkv_ref = bf16[2,16,256,256]{3,2,1,0:T(8,128)(2,1)S(1)} custom-call(bf16[2,16,256,256]{3,2,1,0:T(8,128)(2,1)S(1)} %bitcast.9), custom_call_target="tpu_custom_call" | custom-call | tf_op jit(solution)/shard_map/reduce_all/pallas_call | solution.py:476
  151.5 0.0 copy-start
  151.5 2.0 %copy-done = bf16[2,16,256,256]{3,2,1,0:T(8,128)(2,1)} copy-done((bf16[2,16,256,256]{3,2,1,0:T(8,128)(2,1)}, bf16[2,16,256,256]{3,2,1,0:T(8,128)(2,1)S(1)}, u32[]{:S(2)}) %copy-start) | copy-done | bytes 4194328
  153.5 0.0 all-gather.3.cloned.1.call-done
  153.5 0.0 copy-start.1
  153.5 2.2 %copy-done.1 = bf16[2,16,256,256]{3,2,1,0:T(8,128)(2,1)S(1)} copy-done((bf16[2,16,256,256]{3,2,1,0:T(8,128)(2,1)S(1)}, bf16[2,16,256,256]{3,2,1,0:T(8,128)(2,1)}, u32[]{:S(2)}) %copy-start.1) | copy-done | bytes 4194328
  155.7 0.0 copy-start.6
  155.7 2.2 %copy-done.6 = bf16[256,16,512]{2,1,0:T(8,128)(2,1)S(1)} copy-done((bf16[256,16,512]{2,1,0:T(8,128)(2,1)S(1)}, bf16[256,16,512]{2,1,0:T(8,128)(2,1)}, u32[]{:S(2)}) %copy-start.6) | copy-done | bytes 4194328
  157.9 6.2 %weight_grads.1 = (f32[512,256]{1,0:T(8,128)}, f32[512,256]{1,0:T(8,128)}) custom-call(bf16[16,16,16,512]{3,2,1,0:T(8,128)(2,1)S(1)} %bitcast.8, bf16[2,16,256,256]{3,2,1,0:T(8,128)(2,1)S(1)} %copy-done.1), custom_call_target="tpu_custom_call" | custom-call | tf_op jit(solution)/shard_map/weight_grads/pallas_call | solution.py:515
Async XLA Ops:
  7.2 146.3 %all-gather.3.cloned.1.call-start = ((), (), s32[]{:S(2)}) async-start(), calls=%async_computation.1 | async-start | bytes 4456448 | tf_op jit(solution)/shard_map/all_gather | solution.py:528
  7.2 2.2 %copy-start.4 = (bf16[8192,256]{1,0:T(8,128)(2,1)S(1)}, bf16[8192,256]{1,0:T(8,128)(2,1)}, u32[]{:S(2)}) copy-start(bf16[8192,256]{1,0:T(8,128)(2,1)} %param.8) | copy-start | bytes 12582916
  9.4 2.2 %copy-start.5 = (bf16[8192,256]{1,0:T(8,128)(2,1)S(1)}, bf16[8192,256]{1,0:T(8,128)(2,1)}, u32[]{:S(2)}) copy-start(bf16[8192,256]{1,0:T(8,128)(2,1)} %param.9) | copy-start | bytes 12582916
  11.6 0.9 copy-start.9
  12.5 78.3 %copy-start.10 = (s32[16,2]{0,1:T(2,128)S(1)}, s32[16,2]{0,1:T(2,128)}, u32[]{:S(2)}) copy-start(s32[16,2]{0,1:T(2,128)} %param.10) | copy-start | bytes 388
  12.5 78.4 %copy-start.7 = (bf16[1024,256]{1,0:T(8,128)(2,1)S(1)}, bf16[1024,256]{1,0:T(8,128)(2,1)}, u32[]{:S(2)}) copy-start(bf16[1024,256]{1,0:T(8,128)(2,1)} %q_ref.1) | copy-start | bytes 1572868
  12.5 78.4 %copy-start.8 = (bf16[1024,256]{1,0:T(8,128)(2,1)S(1)}, bf16[1024,256]{1,0:T(8,128)(2,1)}, u32[]{:S(2)}) copy-start(bf16[1024,256]{1,0:T(8,128)(2,1)} %g_ref.1) | copy-start | bytes 1572868
  75.1 2.0 %copy-start.2 = (bf16[2,16,256,256]{3,2,1,0:T(8,128)(2,1)}, bf16[2,16,256,256]{3,2,1,0:T(8,128)(2,1)S(1)}, u32[]{:S(2)}) copy-start(bf16[2,16,256,256]{3,2,1,0:T(8,128)(2,1)S(1)} %get-tuple-element.11) | copy-start | bytes 12582916
  91.0 2.2 %copy-start.3 = (bf16[2,16,256,256]{3,2,1,0:T(8,128)(2,1)S(1)}, bf16[2,16,256,256]{3,2,1,0:T(8,128)(2,1)}, u32[]{:S(2)}) copy-start(bf16[2,16,256,256]{3,2,1,0:T(8,128)(2,1)} %copy-done.2) | copy-start | bytes 12582916
  151.5 2.0 %copy-start = (bf16[2,16,256,256]{3,2,1,0:T(8,128)(2,1)}, bf16[2,16,256,256]{3,2,1,0:T(8,128)(2,1)S(1)}, u32[]{:S(2)}) copy-start(bf16[2,16,256,256]{3,2,1,0:T(8,128)(2,1)S(1)} %reduce_all.1.dkv_ref) | copy-start | bytes 12582916
  153.5 2.2 %copy-start.1 = (bf16[2,16,256,256]{3,2,1,0:T(8,128)(2,1)S(1)}, bf16[2,16,256,256]{3,2,1,0:T(8,128)(2,1)}, u32[]{:S(2)}) copy-start(bf16[2,16,256,256]{3,2,1,0:T(8,128)(2,1)} %copy-done) | copy-start | bytes 12582916
  155.7 2.2 %copy-start.6 = (bf16[256,16,512]{2,1,0:T(8,128)(2,1)S(1)}, bf16[256,16,512]{2,1,0:T(8,128)(2,1)}, u32[]{:S(2)}) copy-start(bf16[256,16,512]{2,1,0:T(8,128)(2,1)} %all-gather.3.cloned.1.call-done) | copy-start | bytes 12582916
Sparse Core Ops, SparseCore 0:
  91.0 37.5 all-gather.2

commit v3 on v2

--- a/solution.py
+++ b/solution.py
@@ -16,6 +16,46 @@
 MESH = pl.DeviceIdType.MESH
 SIDE = 4
 RING = 8
+BATCHES = 4
+ORDER = (
+    ("start", 0), ("start", 1), ("hop", 0, 1, 0, 1), ("hop", 0, 1, 0, -1), ("hop", 0, 1, 1, 1), ("hop", 0, 1, 1, -1),
+    ("twin", 0, -1), ("twin", 0, 1), ("hop", 1, 1, 0, 1), ("hop", 1, 1, 0, -1), ("hop", 1, 1, 1, 1),
+    ("hop", 1, 1, 1, -1), ("twin", 1, -1), ("twin", 1, 1), ("other", 0, -1), ("other", 0, 0), ("own", 0, -1),
+    ("hop", 0, 2, 0, 1), ("hop", 0, 2, 0, -1), ("own", 0, 0), ("own", 0, 1), ("other", 0, 1), ("hop", 0, 2, 1, 1),
+    ("hop", 0, 2, 1, -1), ("twin", 0, -2), ("twin", 0, 2), ("own", 0, -2), ("own", 0, 2), ("other", 1, 0),
+    ("hop", 1, 2, 0, 1), ("hop", 1, 2, 0, -1), ("own", 1, -1), ("own", 1, 0), ("own", 1, 1), ("hop", 1, 2, 1, 1),
+    ("hop", 1, 2, 1, -1), ("twin", 1, -2), ("twin", 1, 2), ("other", 0, -2), ("other", 0, 2), ("hop", 0, 3, 0, 1),
+    ("hop", 0, 3, 0, -1), ("own", 1, -2), ("own", 1, 2), ("other", 1, -1), ("hop", 0, 3, 1, 1), ("hop", 0, 3, 1, -1),
+    ("twin", 0, -3), ("twin", 0, 3), ("own", 0, -3), ("own", 0, 3), ("other", 1, 1), ("hop", 1, 3, 0, 1),
+    ("hop", 1, 3, 0, -1), ("other", 1, -2), ("other", 1, 2), ("own", 2, 0), ("hop", 1, 3, 1, 1), ("twin", 1, -3),
+    ("hop", 1, 3, 1, -1), ("twin", 1, 3), ("other", 0, -3), ("start", 2), ("other", 0, 3), ("hop", 0, 4, 0, 1),
+    ("own", 1, -3), ("own", 1, 3), ("own", 3, 0), ("hop", 0, 4, 1, -1), ("twin", 0, 4), ("own", 0, 4),
+    ("other", 1, -3), ("start", 3), ("hop", 1, 4, 0, 1), ("other", 1, 3), ("other", 2, 0), ("hop", 1, 4, 1, -1),
+    ("twin", 1, 4), ("other", 0, 4), ("project", 0), ("hop", 2, 1, 0, 1), ("hop", 2, 1, 0, -1), ("own", 1, 4),
+    ("hop", 2, 1, 1, 1), ("twin", 2, -1), ("own", 2, -1), ("other", 3, 0), ("hop", 2, 1, 1, -1), ("twin", 2, 1),
+    ("other", 1, 4), ("hop", 3, 1, 0, 1), ("project", 1), ("hop", 3, 1, 0, -1), ("hop", 3, 1, 1, 1), ("twin", 3, -1),
+    ("own", 2, 1), ("other", 2, -1), ("hop", 3, 1, 1, -1), ("twin", 3, 1), ("near1", 0, 0), ("near2", 0, 0),
+    ("relay", 0, 0, 0), ("hop", 2, 2, 0, 1), ("other", 2, 1), ("hop", 2, 2, 0, -1), ("relay", 0, 1, 0),
+    ("near2", 0, 1), ("near1", 0, 1), ("hop", 2, 2, 1, 1), ("twin", 2, -2), ("hop", 2, 2, 1, -1), ("twin", 2, 2),
+    ("own", 2, -2), ("own", 2, 2), ("near1", 1, 0), ("hop", 3, 2, 0, 1), ("near2", 1, 0), ("hop", 3, 2, 0, -1),
+    ("relay", 1, 0, 0), ("own", 3, -1), ("own", 3, 1), ("hop", 3, 2, 1, 1), ("twin", 3, -2), ("relay", 1, 1, 0),
+    ("hop", 3, 2, 1, -1), ("twin", 3, 2), ("near2", 1, 1), ("near1", 1, 1), ("far", 0, 0), ("hop", 2, 3, 0, 1),
+    ("relay", 0, 0, 1), ("other", 2, -2), ("hop", 2, 3, 0, -1), ("other", 2, 2), ("own", 3, -2), ("hop", 2, 3, 1, 1),
+    ("twin", 2, -3), ("relay", 0, 0, 2), ("hop", 2, 3, 1, -1), ("twin", 2, 3), ("relay", 0, 1, 2), ("own", 2, -3),
+    ("own", 2, 3), ("hop", 3, 3, 0, 1), ("far", 0, 1), ("hop", 3, 3, 0, -1), ("relay", 0, 1, 1), ("own", 3, 2),
+    ("other", 3, -1), ("hop", 3, 3, 1, 1), ("twin", 3, -3), ("relay", 1, 0, 1), ("other", 2, -3),
+    ("hop", 3, 3, 1, -1), ("twin", 3, 3), ("far", 1, 0), ("relay", 1, 0, 2), ("hop", 2, 4, 0, 1), ("relay", 1, 1, 2),
+    ("other", 2, 3), ("own", 3, -3), ("own", 3, 3), ("other", 3, 1), ("hop", 2, 4, 1, -1), ("twin", 2, 4),
+    ("far", 1, 1), ("relay", 1, 1, 1), ("own", 2, 4), ("other", 3, -2), ("hop", 3, 4, 0, 1), ("relay", 0, 0, 3),
+    ("other", 3, 2), ("other", 3, -3), ("other", 3, 3), ("other", 2, 4), ("hop", 3, 4, 1, -1), ("twin", 3, 4),
+    ("project", 2), ("relay", 0, 1, 3), ("relay", 1, 0, 3), ("own", 3, 4), ("relay", 1, 1, 3), ("other", 3, 4),
+    ("project", 3), ("swap", 0), ("near1", 2, 0), ("near2", 2, 0), ("relay", 2, 0, 0), ("relay", 2, 1, 0),
+    ("near2", 2, 1), ("near1", 2, 1), ("near2", 3, 0), ("near1", 3, 0), ("relay", 3, 0, 0), ("near1", 3, 1),
+    ("relay", 3, 1, 0), ("near2", 3, 1), ("swap", 1), ("relay", 2, 0, 1), ("far", 2, 0), ("relay", 2, 0, 2),
+    ("relay", 2, 1, 2), ("relay", 2, 1, 1), ("far", 2, 1), ("relay", 3, 1, 1), ("far", 3, 0), ("relay", 3, 0, 2),
+    ("relay", 3, 0, 1), ("far", 3, 1), ("relay", 3, 1, 2), ("relay", 2, 0, 3), ("relay", 3, 0, 3), ("relay", 2, 1, 3),
+    ("relay", 3, 1, 3),
+)
 
 
 def dot_nt(a, b):
@@ -105,32 +145,32 @@
     return context, query_grad, dkv.reshape(kv.shape)
 
 
-def wrap(i, n):
-    return lax.rem(i + n, n)
-
-
 class Place:
     def __init__(self):
         self.seq = lax.axis_index("seq")
         self.head = lax.axis_index("head")
-        self.x, self.y = self.seq // SIDE, lax.rem(self.seq, SIDE)
-        self.z, self.core = self.head // 2, lax.rem(self.head, 2)
+        x, z = lax.div(self.seq, SIDE), lax.div(self.head, 2)
+        y, self.core = self.seq - x * SIDE, self.head - z * 2
+        self.xs = [x] + [lax.rem(x + i, SIDE) for i in range(1, SIDE)]
+        self.ys = [y] + [lax.rem(y + i, SIDE) for i in range(1, SIDE)]
+        self.zs = [z] + [lax.rem(z + i, RING) for i in range(1, RING)]
+        self.pairs = [2 * z for z in self.zs]
+        self.rows = [SIDE * x for x in self.xs]
+        self.other = (self.seq, self.pairs[0] + 1 - self.core)
 
     def along(self, is_x, step):
-        if is_x:
-            return (wrap(self.x + step, SIDE) * SIDE + self.y, self.head)
-        return (self.x * SIDE + wrap(self.y + step, SIDE), self.head)
+        return (self.slot(is_x, step, 0), self.head)
 
     def ring(self, step):
-        return (self.seq, wrap(self.z + step, RING) * 2 + self.core)
+        return (self.seq, self.pairs[step % RING] + self.core)
 
     def twin(self):
-        return (self.seq, self.z * 2 + 1 - self.core)
+        return self.other
 
     def slot(self, first_is_x, first, second):
-        if first_is_x:
-            return wrap(self.x + first, SIDE) * SIDE + wrap(self.y + second, SIDE)
-        return wrap(self.x + second, SIDE) * SIDE + wrap(self.y + first, SIDE)
+        if not first_is_x:
+            first, second = second, first
+        return self.rows[first % SIDE] + self.ys[second % SIDE]
 
 
 def greet(devices):
@@ -194,12 +234,14 @@
         self.send((0, 0), self.fx, -self.sign)
         self.spread(0)
 
-    def near(self):
-        self.wait((-self.sign, 0))
-        self.send((-self.sign, 0), self.fx, self.sign)
-        self.spread(-self.sign)
-        self.wait((self.sign, 0))
-        self.spread(self.sign)
+    def near(self, which):
+        if which == 1:
+            self.wait((-self.sign, 0))
+            self.send((-self.sign, 0), self.fx, self.sign)
+            self.spread(-self.sign)
+        else:
+            self.wait((self.sign, 0))
+            self.spread(self.sign)
 
     def far(self):
         self.wait((-2 * self.sign, 0))
@@ -218,135 +260,184 @@
             self.wait((first, 2))
 
 
-def pool_kernel(states_ref, kw_ref, vw_ref, kv_ref, part_ref, st, w, acc, send_sems, twin_recv, ring_recv, pool_recv, w_sems):
+class Ring:
+    def __init__(self, place, sender, at, ring_recv, twin_recv, rows):
+        self.place, self.sender, self.at = place, sender, at
+        self.ring_recv, self.twin_recv, self.rows = ring_recv, twin_recv, rows
+
+    def slot(self, distance, other):
+        core = 1 - self.place.core if other else self.place.core
+        return self.place.pairs[distance % RING] + core
+
+    def unit(self, slot, b, u):
+        half = self.rows // 2
+        return self.at(slot, b * self.rows + u * half, half)
+
+    def batch(self, slot, b):
+        return self.at(slot, b * self.rows, self.rows)
+
+    def signs(self, d, u):
+        return (1, -1) if d < RING // 2 else ((1,) if u == 0 else (-1,))
+
+    def to_ring(self, slot, b, u, sign):
+        ref = self.unit(slot, b, u)
+        self.sender.send(ref, ref, self.ring_recv.at[slot, 2 * b + u], self.place.ring(sign))
+
+    def to_twin(self, slot, b):
+        ref = self.batch(slot, b)
+        self.sender.send(ref, ref, self.twin_recv.at[slot, b], self.place.twin())
+
+    def start(self, b):
+        for u in range(2):
+            for sign in (1, -1):
+                self.to_ring(self.place.head, b, u, sign)
+        self.to_twin(self.place.head, b)
+
+    def distances(self, d):
+        return (0,) if d == 0 else ((-d, d) if d < RING // 2 else (d,))
+
+    def relay(self, b, d, u, sign):
+        slot = self.slot(-sign * d, False)
+        arrived(self.unit(slot, b, u), self.sender.sems.at[0], self.ring_recv.at[slot, 2 * b + u], self.place.twin())
+        if d < RING // 2 and sign in self.signs(d + 1, u):
+            self.to_ring(slot, b, u, sign)
+
+    def hop(self, b, d):
+        for u in range(2):
+            for sign in self.signs(d, u):
+                self.relay(b, d, u, sign)
+        for distance in self.distances(d):
+            self.to_twin(self.slot(distance, False), b)
+
+    def from_twin(self, b, distance):
+        slot = self.slot(distance, True)
+        arrived(self.batch(slot, b), self.sender.sems.at[0], self.twin_recv.at[slot, b], self.place.twin())
+
+
+def pool_kernel(
+    states_ref, kw_ref, vw_ref, kv_ref, part_ref, st, shares, mid, w, acc,
+    send_sems, twin_recv, ring_recv, pool_recv, swap_recv, w_sems,
+):
     place = Place()
-    heads, rows, feats = st.shape
+    rows, feats = st.shape[1:]
     cols = kv_ref.shape[3]
-    half = rows // 2
+    batches = BATCHES
+    batch = rows // batches
     loads = [pltpu.make_async_copy(kw_ref, w.at[0], w_sems.at[0]), pltpu.make_async_copy(vw_ref, w.at[1], w_sems.at[1])]
     for load in loads:
         load.start()
     st[place.head] = states_ref[...]
     acc[...] = jnp.zeros_like(acc)
-    greet([place.ring(1), place.ring(-1), place.twin()] + [place.along(i, d) for i in (True, False) for d in (1, -1)])
+    greet(
+        [place.ring(1), place.ring(-1), place.twin()]
+        + [place.along(i, d) for i in (True, False) for d in (1, -1, 2)]
+    )
     sender = Sender(send_sems)
 
-    def ref(slot, g):
-        return st.at[slot, pl.ds(g * half, half), :]
-
-    def slot_at(distance, other):
-        core = 1 - place.core if other else place.core
-        return wrap(place.z + distance, RING) * 2 + core
-
-    def to_ring(slot, g, sign):
-        sender.send(ref(slot, g), ref(slot, g), ring_recv.at[slot, g], place.ring(sign))
-
-    def to_twin(slot, g):
-        sender.send(ref(slot, g), ref(slot, g), twin_recv.at[slot, g], place.twin())
-
-    def multiply(slot, g):
-        at = pl.ds(g * half, half)
-        left = st[slot, at, :]
-        acc[at, :cols] += dot_nn(left, w[0, slot])
-        acc[at, cols:] += dot_nn(left, w[1, slot])
-
-    def signs(d, g):
-        return (1, -1) if d < RING // 2 else ((1,) if g == 0 else (-1,))
-
-    def hop(g, d):
-        for sign in signs(d, g):
-            slot = slot_at(-sign * d, False)
-            arrived(ref(slot, g), send_sems.at[0], ring_recv.at[slot, g], place.twin())
-            if sign in signs(d + 1, g) and d < RING // 2:
-                to_ring(slot, g, sign)
-            to_twin(slot, g)
-
-    def own(g, d):
-        for sign in signs(d, g) if d else (1,):
-            multiply(slot_at(-sign * d, False), g)
-
-    def other(g, d):
-        for sign in signs(d, g) if d else (1,):
-            slot = slot_at(-sign * d, True)
-            arrived(ref(slot, g), send_sems.at[0], twin_recv.at[slot, g], place.twin())
-            multiply(slot, g)
-
-    def project(g):
-        at = pl.ds(g * half, half)
-        kv_ref[0, place.seq, at, :] = acc[at, :cols].astype(kv_ref.dtype)
-        kv_ref[1, place.seq, at, :] = acc[at, cols:].astype(kv_ref.dtype)
-
-    def gathers(g):
-        quarter = half // 2
-        return [
-            Gather(place, sender, kv_ref, pool_recv, j, j == 0, 2 * g + i, g * half + i * quarter, quarter, sign)
-            for i, sign in enumerate((1, -1))
+    def at(slot, row, n):
+        return st.at[slot, pl.ds(row, n), :]
+
+    ring = Ring(place, sender, at, ring_recv, twin_recv, batch)
+
+    def multiply(slot, b):
+        here = pl.ds(b * batch, batch)
+        left = st[slot, here, :]
+        acc[here, :cols] += dot_nn(left, w[0, slot])
+        acc[here, cols:] += dot_nn(left, w[1, slot])
+
+    def own(b, distance):
+        multiply(ring.slot(distance, False), b)
+
+    def other(b, distance):
+        ring.from_twin(b, distance)
+        multiply(ring.slot(distance, True), b)
+
+    def twin(b, distance):
+        ring.to_twin(ring.slot(distance, False), b)
+
+    def project(b):
+        here = pl.ds(b * batch, batch)
+        kv_ref[0, place.seq, here, :] = acc[here, :cols].astype(kv_ref.dtype)
+        kv_ref[1, place.seq, here, :] = acc[here, cols:].astype(kv_ref.dtype)
+        for one in gathers[b]:
+            one.begin()
+
+    gathers = [
+        [
+            Gather(place, sender, kv_ref, pool_recv, j, j == 0, b, b * batch, batch, 1 if (b + j) % 2 == 0 else -1)
             for j in range(2)
         ]
-
-    for g in range(2):
-        for sign in (1, -1):
-            to_ring(place.head, g, sign)
-        to_twin(place.head, g)
-    for load in loads:
-        load.wait()
-    hop(0, 1)
-    own(0, 0)
-    hop(1, 1)
-    hop(0, 2)
-    other(0, 0)
-    own(0, 1)
-    hop(1, 2)
-    hop(0, 3)
-    other(0, 1)
-    own(0, 2)
-    hop(1, 3)
-    hop(0, 4)
-    other(0, 2)
-    own(0, 3)
-    other(0, 3)
-    own(0, 4)
-    other(0, 4)
-    project(0)
-    early = gathers(0)
-    for one in early:
-        one.begin()
-    own(1, 0)
-    other(1, 0)
-    own(1, 1)
-    for one in early:
-        one.near()
-    hop(1, 4)
-    other(1, 1)
-    own(1, 2)
-    other(1, 2)
-    for one in early:
-        one.far()
-    own(1, 3)
-    other(1, 3)
-    own(1, 4)
-    other(1, 4)
-    project(1)
-    late = gathers(1)
-    for one in late:
-        one.begin()
-    for i in range(4):
-        for one in early:
-            one.relay(one.relays()[i])
-    for one in late:
-        one.near()
-    for one in late:
-        one.relay(one.relays()[0])
-    for one in late:
-        one.far()
-    mine = pl.ds(pl.multiple_of(place.head * (rows // heads), rows // heads), rows // heads)
-    for slot in range(heads):
-        part_ref[slot] = st[slot, mine, :]
-    for i in range(1, 4):
-        for one in late:
-            one.relay(one.relays()[i])
-    for one in early + late:
-        one.end()
+        for b in range(batches)
+    ]
+
+    share = rows // (SIDE * SIDE)
+    mine = pl.ds(pl.multiple_of(place.head * share, share), share)
+    side = [pl.ds(0, feats // 2), pl.ds(feats // 2, feats // 2)]
+    here = (place.xs, place.ys)
+    steps = (2, 1, -1)
+
+    def gather_share():
+        for slot in range(SIDE * SIDE):
+            x, y = slot // SIDE, slot % SIDE
+            shares[0, x, y] = st[slot, mine, side[0]]
+            shares[1, y, x] = st[slot, mine, side[1]]
+
+    def column(j, source):
+        return part_ref.at[:, source, :, side[j]] if j == 0 else part_ref.at[source, :, :, side[j]]
+
+    def swap_first():
+        gather_share()
+        for i, step in enumerate(steps):
+            for j in range(2):
+                sender.send(
+                    shares.at[j, here[j][step % SIDE]], mid.at[j, here[j][0]], swap_recv.at[j, 0, i],
+                    place.along(j == 0, step),
+                )
+        for j in range(2):
+            mid[j, here[j][0]] = shares[j, here[j][0]]
+
+    def swap_second():
+        for i, step in enumerate(steps):
+            for j in range(2):
+                arrived(mid.at[j, here[j][-step % SIDE]], send_sems.at[0], swap_recv.at[j, 0, i], place.twin())
+        for i, step in enumerate(steps):
+            for j in range(2):
+                sender.send(
+                    mid.at[j, :, here[1 - j][step % SIDE]], column(j, here[1 - j][0]), swap_recv.at[j, 1, i],
+                    place.along(j != 0, step),
+                )
+        for j in range(2):
+            column(j, here[1 - j][0])[...] = mid[j, :, here[1 - j][0]]
+
+    def swap_end():
+        for i, step in enumerate(steps):
+            for j in range(2):
+                arrived(column(j, here[1 - j][-step % SIDE]), send_sems.at[0], swap_recv.at[j, 1, i], place.twin())
+
+    steps_of = {
+        "start": ring.start,
+        "hop": ring.relay,
+        "twin": twin,
+        "own": own,
+        "other": other,
+        "project": project,
+        "near1": lambda b, j: gathers[b][j].near(1),
+        "near2": lambda b, j: gathers[b][j].near(2),
+        "far": lambda b, j: gathers[b][j].far(),
+        "relay": lambda b, j, i: gathers[b][j].relay(gathers[b][j].relays()[i]),
+        "swap": lambda i: (swap_first, swap_second)[i](),
+    }
+    waiting = list(loads)
+    for name, *what in ORDER:
+        if name in ("own", "other") and waiting:
+            for load in waiting:
+                load.wait()
+            waiting = []
+        steps_of[name](*what)
+    swap_end()
+    for b in range(batches):
+        for one in gathers[b]:
+            one.end()
     sender.finish()
 
 
@@ -355,42 +446,55 @@
     cols = key_weight.shape[1]
     heads = key_weight.shape[0] // feats
     seqs = SIDE * SIDE
-    vmem, anywhere = pl.BlockSpec(memory_space=pltpu.VMEM), pl.BlockSpec(memory_space=pl.ANY)
+    share = rows // heads
+    vmem, hbm = pl.BlockSpec(memory_space=pltpu.VMEM), pl.BlockSpec(memory_space=pltpu.HBM)
     dma = pltpu.SemaphoreType.DMA
     return pl.pallas_call(
         pool_kernel,
         out_shape=(
             jax.ShapeDtypeStruct((2, seqs, rows, cols), jnp.bfloat16),
-            jax.ShapeDtypeStruct((heads, rows // heads, feats), jnp.bfloat16),
+            jax.ShapeDtypeStruct((SIDE, SIDE, share, feats), jnp.bfloat16),
         ),
-        in_specs=[vmem, anywhere, anywhere],
+        in_specs=[vmem, hbm, hbm],
         out_specs=(vmem, vmem),
         scratch_shapes=[
             pltpu.VMEM((heads, rows, feats), jnp.bfloat16),
+            pltpu.VMEM((2, SIDE, SIDE, share, feats // 2), jnp.bfloat16),
+            pltpu.VMEM((2, SIDE, SIDE, share, feats // 2), jnp.bfloat16),
             pltpu.VMEM((2, heads, feats, cols), jnp.bfloat16),
             pltpu.VMEM((rows, 2 * cols), jnp.float32),
-            dma((160,)),
-            dma((heads, 2)),
-            dma((heads, 2)),
-            dma((2, seqs, 4)),
+            dma((256,)),
+            dma((heads, BATCHES)),
+            dma((heads, 2 * BATCHES)),
+            dma((2, seqs, BATCHES)),
+            dma((2, 2, 3)),
             dma((2,)),
         ],
         compiler_params=pltpu.CompilerParams(
-            collective_id=1, has_side_effects=True, vmem_limit_bytes=40 * MIB
+            collective_id=1, has_side_effects=True, vmem_limit_bytes=56 * MIB
         ),
         name="pool",
     )(states, key_weight.reshape(heads, feats, cols), value_weight.reshape(heads, feats, cols))
 
 
-def reduce_kernel(dkv_ref, all_ref, box, mid, box2, send_sems, box_recv, box2_recv, pool_recv):
+def reduce_kernel(
+    dkv_ref, part_ref, dk_ref, dv_ref, pooled, t, box, mid, box2,
+    send_sems, box_recv, box2_recv, pool_recv, twin_recv, ring_recv,
+):
     place = Place()
-    rows = dkv_ref.shape[2]
+    rows, cols = dkv_ref.shape[2], dkv_ref.shape[3]
+    heads, feats = t.shape[0], t.shape[2]
+    share = rows // heads
     half = rows // 2
     halves = (pl.ds(0, half), pl.ds(half, half))
     offsets = (2, 1, 3, 0)
-    greet([place.along(i, d) for i in (True, False) for d in (1, -1)])
+    t[place.head] = part_ref[...]
+    greet(
+        [place.along(i, d) for i in (True, False) for d in (1, -1)] + [place.ring(1), place.ring(-1), place.twin()]
+    )
     sender = Sender(send_sems)
     ways = ((0, 1), (1, -1))
+    ring = Ring(place, sender, lambda slot, row, n: t.at[slot, pl.ds(row, n), :], ring_recv, twin_recv, rows)
 
     def add(*terms):
         total = terms[0].astype(jnp.float32)
@@ -418,6 +522,7 @@
         for j in range(2):
             for way, sign in ways:
                 send1(j, way, sign, 1, k, dkv_ref.at[j, place.slot(j == 0, sign, second), halves[1 - way], :])
+    ring.start(0)
     for k, second in enumerate(offsets):
         for j in range(2):
             for way, sign in ways:
@@ -425,6 +530,9 @@
                 mine = dkv_ref[j, place.slot(j == 0, sign, second), halves[way], :]
                 box[j, way, 0, k] = add(box[j, way, 0, k], mine)
                 send1(j, way, sign, 2, k, box.at[j, way, 0, k])
+    dk_ref[...] = jnp.zeros_like(dk_ref)
+    dv_ref[...] = jnp.zeros_like(dv_ref)
+    ring.hop(0, 1)
     for k, second in enumerate(offsets):
         for j in range(2):
             for way, sign in ways:
@@ -438,96 +546,120 @@
             if k in (1, 2):
                 way, sign = ways[k - 1]
                 send2(j, way, sign, 1, mid.at[j, k, halves[1 - way], :])
+        if k == 1:
+            ring.hop(0, 2)
     for j in range(2):
         for way, sign in ways:
             wait2(j, way, 0)
             box2[j, way, 0] = add(box2[j, way, 0], mid[j, 1 + way, halves[way], :])
             send2(j, way, sign, 2, box2.at[j, way, 0])
+    ring.hop(0, 3)
     gathers = []
     for way, sign in ways:
         for j in range(2):
             wait2(j, 1 - way, 1)
             wait2(j, way, 2)
-            all_ref[j, place.seq, halves[way], :] = add(
+            pooled[j, place.seq, halves[way], :] = add(
                 mid[j, 3, halves[way], :], box2[j, 1 - way, 1], box2[j, way, 2]
             )
-            one = Gather(place, sender, all_ref, pool_recv, j, j != 0, way, way * half, half, sign)
+            one = Gather(place, sender, pooled, pool_recv, j, j != 0, way, way * half, half, sign)
             one.begin()
             gathers.append(one)
-    for one in gathers:
-        one.near()
-    for one in gathers:
-        one.relay(one.relays()[0])
-    for one in gathers:
-        one.far()
-    for i in range(1, 4):
+
+    def near():
+        for which in (1, 2):
+            for one in gathers:
+                one.near(which)
+
+    def far():
+        for one in gathers:
+            one.far()
+
+    def relay(i):
         for one in gathers:
             one.relay(one.relays()[i])
-    for one in gathers:
-        one.end()
+
+    def rest(i, second):
+        for one in gathers:
+            one.wait((one.relays()[i], one.sign * second))
+
+    def multiply(x, y):
+        slot = place.slot(True, x, y)
+        left = t[:, pl.ds(pl.multiple_of(slot * share, share), share), :].reshape(rows, feats)
+        right = jnp.concatenate([pooled[0, slot], pooled[1, slot]], axis=1)
+        product = dot_tn(left, right)
+        dk_ref[...] += product[:, :cols]
+        dv_ref[...] += product[:, cols:]
+
+    near()
+    ring.hop(0, 4)
+    relay(0)
+    for distance in range(-RING // 2 + 1, RING // 2 + 1):
+        ring.from_twin(0, distance)
+    multiply(0, 0)
+    far()
+    relay(1)
+    relay(2)
+    rest(0, 1)
+    for step in (1, -1):
+        multiply(step, 0)
+        multiply(0, step)
+    relay(3)
+    rest(0, 2)
+    multiply(2, 0)
+    multiply(0, 2)
+    rest(1, 1)
+    rest(2, 1)
+    for x in (1, -1):
+        for y in (1, -1):
+            multiply(x, y)
+    rest(1, 2)
+    rest(2, 2)
+    rest(3, 1)
+    for step in (1, -1):
+        multiply(step, 2)
+        multiply(2, step)
+    rest(3, 2)
+    multiply(2, 2)
     sender.finish()
 
 
-def reduce_all(dkv):
+def weight_grads(dkv, part):
     _, seqs, rows, cols = dkv.shape
+    feats = part.shape[1]
+    heads = 2 * RING
     half = rows // 2
     vmem = pl.BlockSpec(memory_space=pltpu.VMEM)
     dma = pltpu.SemaphoreType.DMA
     return pl.pallas_call(
         reduce_kernel,
-        out_shape=jax.ShapeDtypeStruct(dkv.shape, jnp.bfloat16),
-        in_specs=[vmem],
-        out_specs=vmem,
+        out_shape=(jax.ShapeDtypeStruct((feats, cols), jnp.float32),) * 2,
+        in_specs=[vmem, vmem],
+        out_specs=(vmem, vmem),
         scratch_shapes=[
+            pltpu.VMEM((2, seqs, rows, cols), jnp.bfloat16),
+            pltpu.VMEM((heads, rows, feats), jnp.bfloat16),
             pltpu.VMEM((2, 2, 3, SIDE, half, cols), jnp.bfloat16),
             pltpu.VMEM((2, SIDE, rows, cols), jnp.bfloat16),
             pltpu.VMEM((2, 2, 3, half, cols), jnp.bfloat16),
-            dma((128,)),
+            dma((192,)),
             dma((2, 2, 3, SIDE)),
             dma((2, 2, 3)),
             dma((2, seqs, 2)),
+            dma((heads, 1)),
+            dma((heads, 2)),
         ],
         compiler_params=pltpu.CompilerParams(
             collective_id=2, has_side_effects=True, vmem_limit_bytes=32 * MIB
         ),
         name="reduce_all",
-    )(dkv)
-
-
-def weight_kernel(t_ref, dkv_ref, dk_ref, dv_ref):
-    heads, seqs, rows, feats = t_ref.shape
-    dk_ref[...] = jnp.zeros_like(dk_ref)
-    dv_ref[...] = jnp.zeros_like(dv_ref)
-
-    def block(s, _):
-        left = t_ref[:, pl.ds(s, 1), :, :].reshape(heads * rows, feats)
-        dk_ref[...] += dot_tn(left, dkv_ref[0, s])
-        dv_ref[...] += dot_tn(left, dkv_ref[1, s])
-        return 0
-
-    lax.fori_loop(0, seqs, block, 0)
-
-
-def weight_grads(t, dkv):
-    heads, seqs, rows, feats = t.shape
-    cols = dkv.shape[3]
-    vmem = pl.BlockSpec(memory_space=pltpu.VMEM)
-    return pl.pallas_call(
-        weight_kernel,
-        out_shape=(jax.ShapeDtypeStruct((feats, cols), jnp.float32),) * 2,
-        in_specs=[vmem, vmem],
-        out_specs=(vmem, vmem),
-        compiler_params=pltpu.CompilerParams(vmem_limit_bytes=24 * MIB),
-        name="weight_grads",
-    )(t, dkv)
+    )(dkv, part)
 
 
 def local(queries, states, key_weight, value_weight, neighbour_ids, out_grad):
     kv, part = pool(states, key_weight, value_weight)
-    column = lax.all_to_all(part, "seq", split_axis=0, concat_axis=0, tiled=True)
-    t = lax.all_gather(column, "head", axis=0, tiled=False)
     context, query_grad, dkv = attend(neighbour_ids, queries, out_grad, kv)
-    dk, dv = weight_grads(t, reduce_all(dkv))
+    dk, dv = weight_grads(dkv, part.reshape(states.shape))
     return context, query_grad, dk, dv
 
 

time: 172 us -> 136 us (0.79)
  blocking collectives: 13.8 us -> 0 us
  between operations: 14.1 us -> 0.67 us
  local copies, waits for them, and re-layouts: 15.9 us -> 4.54 us
  Pallas kernels: 127 us -> 131 us
    all_to_all x1 -> x0, blocking collectives: 13.8 us -> none  [local(): lax.all_to_all(part, 'seq', split_axis=0, concat_axis=0, tiled=True)]
    unnamed x23 -> x11, local copies, waits for them, and re-layouts: 15.9 us -> 4.54 us
    pallas_call x2 -> x1, Pallas kernels: 50.6 us -> 52.7 us  [weight_grads(): pl.pallas_call(reduce_kernel, out_shape=(jax.ShapeDtypeStruct((feats, col...]
    pallas_call x1, Pallas kernels: 62.5 us -> 64.3 us  [pool(): pl.pallas_call(pool_kernel, out_shape=(jax.ShapeDtypeStruct((2, seqs, row...]
  transfers between devices with their start and end apart: 1 -> 0, of which waited for: 0 -> 0; matrix products, arithmetic and copies ran while one was open for 0% -> 0% of each run, Pallas kernels for 34% -> 0%
where the time goes in v3:
time: 136 us
  Pallas kernels  131 us (96%)
  local copies, waits for them, and re-layouts  4.54 us (3%)
    pallas_call x1, Pallas kernels, pool(): pl.pallas_call(pool_kernel, out_shape=(jax.ShapeDtypeStruct((2, seqs, row...  64.3 us
    pallas_call x1, Pallas kernels, weight_grads(): pl.pallas_call(reduce_kernel, out_shape=(jax.ShapeDtypeStruct((feats, col...  52.7 us
    pallas_call x1, Pallas kernels, attend(): pl.pallas_call(attend_kernel, out_shape=(jax.ShapeDtypeStruct((rows, cols...  14.1 us
    unnamed x11, local copies, waits for them, and re-layouts  4.54 us

profile of v3, /device:TPU:2, one launch (start us, length us, event | category | flops | bytes accessed | tf_op | source)
XLA Modules:
  0.0 136.3 jit_solution(7798717152119380272)
XLA Ops:
  0.6 0.8 copy.10.ids_ref
  1.4 0.0 copy-start.1
  1.4 0.0 copy-start.2
  1.4 64.3 %pool.1 = (bf16[2,16,256,256]{3,2,1,0:T(8,128)(2,1)}, bf16[4,4,16,512]{3,2,1,0:T(8,128)(2,1)}) custom-call(bf16[256,512]{1,0:T(8,128)(2,1)} %states_ref.1, bf16[16,512,256]{2,1,0:T(8,128)(2,1)} %bitcast.8, bf16[16,512,256]{2,1,0:T(8,128)(2,1)} %bitcast.9), custom_call_target="tpu_custom_call" | custom-call | tf_op jit(solution)/shard_map/pool/pallas_call | solution.py:452
  65.7 0.0 copy-done.1
  65.7 0.0 copy-done.2
  65.7 0.0 copy-start
  65.7 2.2 %copy-done = bf16[2,16,256,256]{3,2,1,0:T(8,128)(2,1)S(1)} copy-done((bf16[2,16,256,256]{3,2,1,0:T(8,128)(2,1)S(1)}, bf16[2,16,256,256]{3,2,1,0:T(8,128)(2,1)}, u32[]{:S(2)}) %copy-start) | copy-done | bytes 4194328
  67.9 0.0 copy-start.3
  67.9 14.1 %attend.1 = (bf16[1024,256]{1,0:T(8,128)(2,1)}, bf16[1024,256]{1,0:T(8,128)(2,1)}, bf16[2,32,128,256]{3,2,1,0:T(8,128)(2,1)S(1)}) custom-call(s32[16,2]{1,0:T(8,128)S(1)} %copy.10.ids_ref, bf16[1024,256]{1,0:T(8,128)(2,1)S(1)} %copy-done.1, bf16[1024,256]{1,0:T(8,128)(2,1)S(1)} %copy-done.2, bf16[2,32,128,256]{3,2,1,0:T(8,128)(2,1)S(1)} %bitcast.5), custom_call_target="tpu_custom_call" | custom-call | tf_op jit(solution)/shard_map/attend/pallas_call | solution.py:132
  82.0 0.0 copy-done.3
  82.0 52.7 %reduce_all.1 = (f32[512,256]{1,0:T(8,128)S(1)}, f32[512,256]{1,0:T(8,128)S(1)}) custom-call(bf16[2,16,256,256]{3,2,1,0:T(8,128)(2,1)S(1)} %bitcast.6, bf16[256,512]{1,0:T(8,128)(2,1)S(1)} %bitcast.7), custom_call_target="tpu_custom_call" | custom-call | tf_op jit(solution)/shard_map/reduce_all/pallas_call | solution.py:634
  134.7 0.8 copy.13
  135.5 0.8 copy.14
Async XLA Ops:
  1.4 64.3 %copy-start.1 = (bf16[1024,256]{1,0:T(8,128)(2,1)S(1)}, bf16[1024,256]{1,0:T(8,128)(2,1)}, u32[]{:S(2)}) copy-start(bf16[1024,256]{1,0:T(8,128)(2,1)} %q_ref.1) | copy-start | bytes 1572868
  1.4 64.3 %copy-start.2 = (bf16[1024,256]{1,0:T(8,128)(2,1)S(1)}, bf16[1024,256]{1,0:T(8,128)(2,1)}, u32[]{:S(2)}) copy-start(bf16[1024,256]{1,0:T(8,128)(2,1)} %g_ref.1) | copy-start | bytes 1572868
  65.7 2.2 %copy-start = (bf16[2,16,256,256]{3,2,1,0:T(8,128)(2,1)S(1)}, bf16[2,16,256,256]{3,2,1,0:T(8,128)(2,1)}, u32[]{:S(2)}) copy-start(bf16[2,16,256,256]{3,2,1,0:T(8,128)(2,1)} %get-tuple-element.11) | copy-start | bytes 12582916
  67.9 14.1 %copy-start.3 = (bf16[4,4,16,512]{3,2,1,0:T(8,128)(2,1)S(1)}, bf16[4,4,16,512]{3,2,1,0:T(8,128)(2,1)}, u32[]{:S(2)}) copy-start(bf16[4,4,16,512]{3,2,1,0:T(8,128)(2,1)} %get-tuple-element.15) | copy-start | bytes 786436

commit v4 on v3

--- a/solution.py
+++ b/solution.py
@@ -92,7 +92,7 @@
 
     def span(c, _):
         rows = pl.ds(c * SPAN, SPAN)
-        id0, id1 = ids_ref[c, 0], ids_ref[c, 1]
+        id0, id1 = ids_ref[0, c], ids_ref[1, c]
         keys = jnp.concatenate([kv_ref[0, id0], kv_ref[0, id1]], axis=0)
         values = jnp.concatenate([kv_ref[1, id0], kv_ref[1, id1]], axis=0)
         q2 = stack(q_ref[rows, :])
@@ -115,7 +115,7 @@
         acc_ref[1, id1] += dv[NBR:]
         return 0
 
-    lax.fori_loop(0, spans, span, 0)
+    lax.fori_loop(0, spans, span, 0, unroll=4)
 
     def store(i, _):
         for j in range(2):
@@ -182,23 +182,27 @@
 
 class Sender:
     def __init__(self, sems):
-        self.sems, self.started = sems, []
-
-    def send(self, src, dst, recv_sem, device):
-        copy = pltpu.make_async_remote_copy(
+        self.sems = sems
+
+    def send(self, src, dst, group, recv_sem, device):
+        pltpu.make_async_remote_copy(
             src_ref=src,
             dst_ref=dst,
-            send_sem=self.sems.at[len(self.started)],
+            send_sem=self.sems.at[group],
             recv_sem=recv_sem,
             device_id=device,
             device_id_type=MESH,
-        )
-        copy.start()
-        self.started.append(copy)
-
-    def finish(self):
-        for copy in self.started:
-            copy.wait_send()
+        ).start()
+
+    def finish(self, ref, group, recv_sem, device):
+        pltpu.make_async_remote_copy(
+            src_ref=ref,
+            dst_ref=ref,
+            send_sem=self.sems.at[group],
+            recv_sem=recv_sem,
+            device_id=device,
+            device_id_type=MESH,
+        ).wait_send()
 
 
 def arrived(ref, send_sem, recv_sem, device):
@@ -208,61 +212,61 @@
 
 
 class Gather:
-    def __init__(self, place, sender, buf, recv, j, first_is_x, cid, row, rows, sign):
-        self.place, self.sender, self.buf, self.recv = place, sender, buf, recv
-        self.j, self.fx, self.cid, self.row, self.rows, self.sign = j, first_is_x, cid, row, rows, sign
+    def __init__(self, place, sender, group, buf, recv, j, first_is_x, row, rows, sign, together):
+        self.place, self.sender, self.group, self.buf, self.recv = place, sender, group, buf, recv
+        self.j, self.fx, self.row, self.rows, self.sign, self.together = j, first_is_x, row, rows, sign, together
 
     def ref(self, slot):
         return self.buf.at[self.j, slot, pl.ds(self.row, self.rows), :]
 
-    def send(self, offsets, is_x, step):
+    def send(self, offsets, kind, is_x, step):
         slot = self.place.slot(self.fx, *offsets)
-        self.sender.send(
-            self.ref(slot), self.ref(slot), self.recv.at[self.j, slot, self.cid], self.place.along(is_x, step)
-        )
-
-    def wait(self, offsets):
-        slot = self.place.slot(self.fx, *offsets)
-        arrived(self.ref(slot), self.sender.sems.at[0], self.recv.at[self.j, slot, self.cid], self.place.twin())
-
-    def spread(self, first):
-        self.send((first, 0), not self.fx, self.sign)
-        self.send((first, 0), not self.fx, -self.sign)
+        self.sender.send(self.ref(slot), self.ref(slot), self.group, self.recv(kind), self.place.along(is_x, step))
+
+    def wait(self, offsets, kind):
+        ref = self.ref(self.place.slot(self.fx, *offsets))
+        arrived(ref, self.sender.sems.at[0], self.recv(kind), self.place.twin())
+
+    def relays(self):
+        return [0, -self.sign, self.sign, 2]
+
+    def last(self, i, second):
+        return 7 if self.together else 7 + 2 * i + second - 1
+
+    def spread(self, i):
+        first = self.relays()[i]
+        self.send((first, 0), 3 + i, not self.fx, self.sign)
+        self.send((first, 0), self.last(i, 1), not self.fx, -self.sign)
 
     def begin(self):
-        self.send((0, 0), self.fx, self.sign)
-        self.send((0, 0), self.fx, -self.sign)
+        self.send((0, 0), 0, self.fx, self.sign)
+        self.send((0, 0), 1, self.fx, -self.sign)
         self.spread(0)
 
     def near(self, which):
         if which == 1:
-            self.wait((-self.sign, 0))
-            self.send((-self.sign, 0), self.fx, self.sign)
-            self.spread(-self.sign)
+            self.wait((-self.sign, 0), 0)
+            self.send((-self.sign, 0), 2, self.fx, self.sign)
         else:
-            self.wait((self.sign, 0))
-            self.spread(self.sign)
+            self.wait((self.sign, 0), 1)
+        self.spread(which)
 
     def far(self):
-        self.wait((-2 * self.sign, 0))
-        self.spread(2)
-
-    def relay(self, first):
-        self.wait((first, -self.sign))
-        self.send((first, -self.sign), not self.fx, self.sign)
-
-    def relays(self):
-        return [0, -self.sign, self.sign, 2]
-
-    def end(self):
-        for first in self.relays():
-            self.wait((first, self.sign))
-            self.wait((first, 2))
+        self.wait((-2 * self.sign, 0), 2)
+        self.spread(3)
+
+    def relay(self, i):
+        first = self.relays()[i]
+        self.wait((first, -self.sign), 3 + i)
+        self.send((first, -self.sign), self.last(i, 2), not self.fx, self.sign)
+
+    def rest(self, i, second):
+        self.wait((self.relays()[i], self.sign * second), self.last(i, second))
 
 
 class Ring:
-    def __init__(self, place, sender, at, ring_recv, twin_recv, rows):
-        self.place, self.sender, self.at = place, sender, at
+    def __init__(self, place, sender, groups, at, ring_recv, twin_recv, rows):
+        self.place, self.sender, self.groups, self.at = place, sender, groups, at
         self.ring_recv, self.twin_recv, self.rows = ring_recv, twin_recv, rows
 
     def slot(self, distance, other):
@@ -279,39 +283,39 @@
     def signs(self, d, u):
         return (1, -1) if d < RING // 2 else ((1,) if u == 0 else (-1,))
 
-    def to_ring(self, slot, b, u, sign):
+    def ring_sem(self, sign, d, b, u):
+        return self.ring_recv.at[0 if sign > 0 else 1, d - 1, 2 * b + u]
+
+    def to_ring(self, slot, d, b, u, sign):
         ref = self.unit(slot, b, u)
-        self.sender.send(ref, ref, self.ring_recv.at[slot, 2 * b + u], self.place.ring(sign))
-
-    def to_twin(self, slot, b):
-        ref = self.batch(slot, b)
-        self.sender.send(ref, ref, self.twin_recv.at[slot, b], self.place.twin())
+        self.sender.send(ref, ref, self.groups[0] + b, self.ring_sem(sign, d, b, u), self.place.ring(sign))
+
+    def to_twin(self, distance, b):
+        ref = self.batch(self.slot(distance, False), b)
+        self.sender.send(ref, ref, self.groups[1] + b, self.twin_recv(distance, b), self.place.twin())
 
     def start(self, b):
         for u in range(2):
             for sign in (1, -1):
-                self.to_ring(self.place.head, b, u, sign)
-        self.to_twin(self.place.head, b)
-
-    def distances(self, d):
-        return (0,) if d == 0 else ((-d, d) if d < RING // 2 else (d,))
+                self.to_ring(self.place.head, 1, b, u, sign)
+        self.to_twin(0, b)
 
     def relay(self, b, d, u, sign):
         slot = self.slot(-sign * d, False)
-        arrived(self.unit(slot, b, u), self.sender.sems.at[0], self.ring_recv.at[slot, 2 * b + u], self.place.twin())
+        arrived(self.unit(slot, b, u), self.sender.sems.at[0], self.ring_sem(sign, d, b, u), self.place.twin())
         if d < RING // 2 and sign in self.signs(d + 1, u):
-            self.to_ring(slot, b, u, sign)
+            self.to_ring(slot, d + 1, b, u, sign)
 
     def hop(self, b, d):
         for u in range(2):
             for sign in self.signs(d, u):
                 self.relay(b, d, u, sign)
-        for distance in self.distances(d):
-            self.to_twin(self.slot(distance, False), b)
+        for distance in (-d, d) if d < RING // 2 else (d,):
+            self.to_twin(distance, b)
 
     def from_twin(self, b, distance):
         slot = self.slot(distance, True)
-        arrived(self.batch(slot, b), self.sender.sems.at[0], self.twin_recv.at[slot, b], self.place.twin())
+        arrived(self.batch(slot, b), self.sender.sems.at[0], self.twin_recv(distance, b), self.place.twin())
 
 
 def pool_kernel(
@@ -337,7 +341,10 @@
     def at(slot, row, n):
         return st.at[slot, pl.ds(row, n), :]
 
-    ring = Ring(place, sender, at, ring_recv, twin_recv, batch)
+    def twin_sem(distance, b):
+        return twin_recv.at[distance + RING // 2 - 1, b]
+
+    ring = Ring(place, sender, (0, batches), at, ring_recv, twin_sem, batch)
 
     def multiply(slot, b):
         here = pl.ds(b * batch, batch)
@@ -353,7 +360,7 @@
         multiply(ring.slot(distance, True), b)
 
     def twin(b, distance):
-        ring.to_twin(ring.slot(distance, False), b)
+        ring.to_twin(distance, b)
 
     def project(b):
         here = pl.ds(b * batch, batch)
@@ -362,13 +369,12 @@
         for one in gathers[b]:
             one.begin()
 
-    gathers = [
-        [
-            Gather(place, sender, kv_ref, pool_recv, j, j == 0, b, b * batch, batch, 1 if (b + j) % 2 == 0 else -1)
-            for j in range(2)
-        ]
-        for b in range(batches)
-    ]
+    def gather(b, j):
+        sign = 1 if (b + j) % 2 == 0 else -1
+        recv = lambda kind: pool_recv.at[b, j, kind]
+        return Gather(place, sender, 2 * batches + b, kv_ref, recv, j, j == 0, b * batch, batch, sign, True)
+
+    gathers = [[gather(b, j) for j in range(2)] for b in range(batches)]
 
     share = rows // (SIDE * SIDE)
     mine = pl.ds(pl.multiple_of(place.head * share, share), share)
@@ -390,8 +396,8 @@
         for i, step in enumerate(steps):
             for j in range(2):
                 sender.send(
-                    shares.at[j, here[j][step % SIDE]], mid.at[j, here[j][0]], swap_recv.at[j, 0, i],
-                    place.along(j == 0, step),
+                    shares.at[j, here[j][step % SIDE]], mid.at[j, here[j][0]], 3 * batches,
+                    swap_recv.at[j, 0, i], place.along(j == 0, step),
                 )
         for j in range(2):
             mid[j, here[j][0]] = shares[j, here[j][0]]
@@ -403,8 +409,8 @@
         for i, step in enumerate(steps):
             for j in range(2):
                 sender.send(
-                    mid.at[j, :, here[1 - j][step % SIDE]], column(j, here[1 - j][0]), swap_recv.at[j, 1, i],
-                    place.along(j != 0, step),
+                    mid.at[j, :, here[1 - j][step % SIDE]], column(j, here[1 - j][0]), 3 * batches,
+                    swap_recv.at[j, 1, i], place.along(j != 0, step),
                 )
         for j in range(2):
             column(j, here[1 - j][0])[...] = mid[j, :, here[1 - j][0]]
@@ -424,7 +430,7 @@
         "near1": lambda b, j: gathers[b][j].near(1),
         "near2": lambda b, j: gathers[b][j].near(2),
         "far": lambda b, j: gathers[b][j].far(),
-        "relay": lambda b, j, i: gathers[b][j].relay(gathers[b][j].relays()[i]),
+        "relay": lambda b, j, i: gathers[b][j].relay(i),
         "swap": lambda i: (swap_first, swap_second)[i](),
     }
     waiting = list(loads)
@@ -436,9 +442,14 @@
         steps_of[name](*what)
     swap_end()
     for b in range(batches):
-        for one in gathers[b]:
-            one.end()
-    sender.finish()
+        for j in range(2):
+            arrived(kv_ref.at[j, pl.ds(0, 8), pl.ds(0, batch), :], send_sems.at[0], pool_recv.at[b, j, 7], place.twin())
+    spare = (swap_recv.at[0, 0, 0], place.twin())
+    for b in range(batches):
+        sender.finish(st.at[pl.ds(0, RING - 1), pl.ds(0, batch), :], b, *spare)
+        sender.finish(st.at[pl.ds(0, RING), pl.ds(0, batch), :], batches + b, *spare)
+        sender.finish(kv_ref.at[0, pl.ds(0, 15), pl.ds(0, 2 * batch), :], 2 * batches + b, *spare)
+    sender.finish(st.at[pl.ds(0, 6), pl.ds(0, SIDE * share), :], 3 * batches, *spare)
 
 
 def pool(states, key_weight, value_weight):
@@ -463,15 +474,15 @@
             pltpu.VMEM((2, SIDE, SIDE, share, feats // 2), jnp.bfloat16),
             pltpu.VMEM((2, heads, feats, cols), jnp.bfloat16),
             pltpu.VMEM((rows, 2 * cols), jnp.float32),
-            dma((256,)),
-            dma((heads, BATCHES)),
-            dma((heads, 2 * BATCHES)),
-            dma((2, seqs, BATCHES)),
+            dma((3 * BATCHES + 1,)),
+            dma((RING, BATCHES)),
+            dma((2, RING // 2, 2 * BATCHES)),
+            dma((BATCHES, 2, 8)),
             dma((2, 2, 3)),
             dma((2,)),
         ],
         compiler_params=pltpu.CompilerParams(
-            collective_id=1, has_side_effects=True, vmem_limit_bytes=56 * MIB
+            collective_id=1, has_side_effects=True, vmem_limit_bytes=48 * MIB
         ),
         name="pool",
     )(states, key_weight.reshape(heads, feats, cols), value_weight.reshape(heads, feats, cols))
@@ -494,7 +505,10 @@
     )
     sender = Sender(send_sems)
     ways = ((0, 1), (1, -1))
-    ring = Ring(place, sender, lambda slot, row, n: t.at[slot, pl.ds(row, n), :], ring_recv, twin_recv, rows)
+    ring = Ring(
+        place, sender, (4, 5), lambda slot, row, n: t.at[slot, pl.ds(row, n), :], ring_recv,
+        lambda distance, b: twin_recv.at[0], rows,
+    )
 
     def add(*terms):
         total = terms[0].astype(jnp.float32)
@@ -503,13 +517,13 @@
         return total.astype(jnp.bfloat16)
 
     def send1(j, way, sign, kind, k, src):
-        sender.send(src, box.at[j, way, kind, k], box_recv.at[j, way, kind, k], place.along(j == 0, sign))
+        sender.send(src, box.at[j, way, kind, k], 0, box_recv.at[j, way, kind, k], place.along(j == 0, sign))
 
     def wait1(j, way, kind, k):
         arrived(box.at[j, way, kind, k], send_sems.at[0], box_recv.at[j, way, kind, k], place.along(j == 0, 1))
 
     def send2(j, way, sign, kind, src):
-        sender.send(src, box2.at[j, way, kind], box2_recv.at[j, way, kind], place.along(j != 0, sign))
+        sender.send(src, box2.at[j, way, kind], 1, box2_recv.at[j, way, kind], place.along(j != 0, sign))
 
     def wait2(j, way, kind):
         arrived(box2.at[j, way, kind], send_sems.at[0], box2_recv.at[j, way, kind], place.along(j != 0, 1))
@@ -554,6 +568,11 @@
             box2[j, way, 0] = add(box2[j, way, 0], mid[j, 1 + way, halves[way], :])
             send2(j, way, sign, 2, box2.at[j, way, 0])
     ring.hop(0, 3)
+
+    def gather(way, sign, j):
+        recv = lambda kind: pool_recv.at[way, j, kind]
+        return Gather(place, sender, 2 + j, pooled, recv, j, j != 0, way * half, half, sign, False)
+
     gathers = []
     for way, sign in ways:
         for j in range(2):
@@ -562,9 +581,8 @@
             pooled[j, place.seq, halves[way], :] = add(
                 mid[j, 3, halves[way], :], box2[j, 1 - way, 1], box2[j, way, 2]
             )
-            one = Gather(place, sender, pooled, pool_recv, j, j != 0, way, way * half, half, sign)
-            one.begin()
-            gathers.append(one)
+            gathers.append(gather(way, sign, j))
+            gathers[-1].begin()
 
     def near():
         for which in (1, 2):
@@ -577,11 +595,11 @@
 
     def relay(i):
         for one in gathers:
-            one.relay(one.relays()[i])
+            one.relay(i)
 
     def rest(i, second):
         for one in gathers:
-            one.wait((one.relays()[i], one.sign * second))
+            one.rest(i, second)
 
     def multiply(x, y):
         slot = place.slot(True, x, y)
@@ -594,8 +612,7 @@
     near()
     ring.hop(0, 4)
     relay(0)
-    for distance in range(-RING // 2 + 1, RING // 2 + 1):
-        ring.from_twin(0, distance)
+    arrived(t.at[pl.ds(0, RING)], send_sems.at[0], twin_recv.at[0], place.twin())
     multiply(0, 0)
     far()
     relay(1)
@@ -621,7 +638,13 @@
         multiply(2, step)
     rest(3, 2)
     multiply(2, 2)
-    sender.finish()
+    spare = (twin_recv.at[0], place.twin())
+    sender.finish(box, 0, *spare)
+    sender.finish(box2, 1, *spare)
+    for j in range(2):
+        sender.finish(pooled.at[j, pl.ds(0, 15)], 2 + j, *spare)
+    sender.finish(t.at[pl.ds(0, RING - 1)], 4, *spare)
+    sender.finish(t.at[pl.ds(0, RING)], 5, *spare)
 
 
 def weight_grads(dkv, part):
@@ -642,12 +665,12 @@
             pltpu.VMEM((2, 2, 3, SIDE, half, cols), jnp.bfloat16),
             pltpu.VMEM((2, SIDE, rows, cols), jnp.bfloat16),
             pltpu.VMEM((2, 2, 3, half, cols), jnp.bfloat16),
-            dma((192,)),
+            dma((6,)),
             dma((2, 2, 3, SIDE)),
             dma((2, 2, 3)),
-            dma((2, seqs, 2)),
-            dma((heads, 1)),
-            dma((heads, 2)),
+            dma((2, 2, 15)),
+            dma((1,)),
+            dma((2, RING // 2, 2)),
         ],
         compiler_params=pltpu.CompilerParams(
             collective_id=2, has_side_effects=True, vmem_limit_bytes=32 * MIB
@@ -658,7 +681,7 @@
 
 def local(queries, states, key_weight, value_weight, neighbour_ids, out_grad):
     kv, part = pool(states, key_weight, value_weight)
-    context, query_grad, dkv = attend(neighbour_ids, queries, out_grad, kv)
+    context, query_grad, dkv = attend(neighbour_ids.T, queries, out_grad, kv)
     dk, dv = weight_grads(dkv, part.reshape(states.shape))
     return context, query_grad, dk, dv
 

time: 136 us -> 123 us (0.904)
  Pallas kernels: 131 us -> 120 us
  local copies, waits for them, and re-layouts: 4.54 us -> 2.54 us
    pallas_call x1, Pallas kernels: 64.3 us -> 57.3 us  [pool(): pl.pallas_call(pool_kernel, out_shape=(jax.ShapeDtypeStruct((2, seqs, row...]
    pallas_call x1, Pallas kernels: 14.1 us -> 11.7 us  [attend(): pl.pallas_call(attend_kernel, out_shape=(jax.ShapeDtypeStruct((rows, cols...]
    pallas_call x1, Pallas kernels: 52.7 us -> 50.5 us  [weight_grads(): pl.pallas_call(reduce_kernel, out_shape=(jax.ShapeDtypeStruct((feats, col...]
    unnamed x11 -> x10, local copies, waits for them, and re-layouts: 4.54 us -> 2.54 us
where the time goes in v4:
time: 123 us
  Pallas kernels  120 us (98%)
  local copies, waits for them, and re-layouts  2.54 us (2%)
    pallas_call x1, Pallas kernels, pool(): pl.pallas_call(pool_kernel, out_shape=(jax.ShapeDtypeStruct((2, seqs, row...  57.3 us
    pallas_call x1, Pallas kernels, weight_grads(): pl.pallas_call(reduce_kernel, out_shape=(jax.ShapeDtypeStruct((feats, col...  50.5 us
    pallas_call x1, Pallas kernels, attend(): pl.pallas_call(attend_kernel, out_shape=(jax.ShapeDtypeStruct((rows, cols...  11.7 us
    unnamed x10, local copies, waits for them, and re-layouts  2.54 us

profile of v4, /device:TPU:2, one launch (start us, length us, event | category | flops | bytes accessed | tf_op | source)
XLA Modules:
  0.0 122.7 jit_solution(15811006105534506882)
XLA Ops:
  0.6 0.0 copy-start.2
  0.6 0.9 copy-done.2
  1.6 0.0 copy-start
  1.6 0.0 copy-start.1
  1.6 0.0 copy-start.3
  1.6 57.3 %pool.1 = (bf16[2,16,256,256]{3,2,1,0:T(8,128)(2,1)S(1)}, bf16[4,4,16,512]{3,2,1,0:T(8,128)(2,1)S(1)}) custom-call(bf16[256,512]{1,0:T(8,128)(2,1)S(1)} %copy-done.2, bf16[16,512,256]{2,1,0:T(8,128)(2,1)} %bitcast.10, bf16[16,512,256]{2,1,0:T(8,128)(2,1)} %bitcast.11), custom_call_target="tpu_custom_call" | custom-call | tf_op jit(solution)/shard_map/pool/pallas_call | solution.py:463
  58.9 0.0 copy-done
  58.9 0.0 copy-done.1
  58.9 0.0 copy-done.3
  58.9 11.7 %attend.1 = (bf16[1024,256]{1,0:T(8,128)(2,1)}, bf16[1024,256]{1,0:T(8,128)(2,1)}, bf16[2,32,128,256]{3,2,1,0:T(8,128)(2,1)S(1)}) custom-call(s32[2,16]{1,0:T(2,128)S(1)} %bitcast.9, bf16[1024,256]{1,0:T(8,128)(2,1)S(1)} %copy-done, bf16[1024,256]{1,0:T(8,128)(2,1)S(1)} %copy-done.1, bf16[2,32,128,256]{3,2,1,0:T(8,128)(2,1)S(1)} %bitcast.7), custom_call_target="tpu_custom_call" | custom-call | tf_op jit(solution)/shard_map/attend/pallas_call | solution.py:132
  70.6 50.5 %reduce_all.1 = (f32[512,256]{1,0:T(8,128)S(1)}, f32[512,256]{1,0:T(8,128)S(1)}) custom-call(bf16[2,16,256,256]{3,2,1,0:T(8,128)(2,1)S(1)} %bitcast.6, bf16[256,512]{1,0:T(8,128)(2,1)S(1)} %bitcast.8), custom_call_target="tpu_custom_call" | custom-call | tf_op jit(solution)/shard_map/reduce_all/pallas_call | solution.py:657
  121.1 0.8 copy.12
  121.9 0.8 copy.13
Async XLA Ops:
  0.6 1.0 copy-start.2
  1.6 57.3 %copy-start = (bf16[1024,256]{1,0:T(8,128)(2,1)S(1)}, bf16[1024,256]{1,0:T(8,128)(2,1)}, u32[]{:S(2)}) copy-start(bf16[1024,256]{1,0:T(8,128)(2,1)} %q_ref.1) | copy-start | bytes 1572868
  1.6 57.3 %copy-start.1 = (bf16[1024,256]{1,0:T(8,128)(2,1)S(1)}, bf16[1024,256]{1,0:T(8,128)(2,1)}, u32[]{:S(2)}) copy-start(bf16[1024,256]{1,0:T(8,128)(2,1)} %g_ref.1) | copy-start | bytes 1572868
  1.6 57.3 %copy-start.3 = (s32[16,2]{0,1:T(2,128)S(1)}, s32[16,2]{0,1:T(2,128)}, u32[]{:S(2)}) copy-start(s32[16,2]{0,1:T(2,128)} %param.10) | copy-start | bytes 388

commit v5 on v4

--- a/solution.py
+++ b/solution.py
@@ -101,7 +101,7 @@
         prob_grad = dot_nt(g2, values)
         top = jnp.max(scores, axis=-1, keepdims=True)
         e = jnp.exp(scores - top)
-        probs = e / jnp.sum(e, axis=-1, keepdims=True)
+        probs = e * (1.0 / jnp.sum(e, axis=-1, keepdims=True))
         low = probs.astype(jnp.bfloat16)
         delta = jnp.sum(probs * prob_grad, axis=-1, keepdims=True)
         sg = (probs * (prob_grad - delta) * SCALE).astype(jnp.bfloat16)
@@ -115,7 +115,7 @@
         acc_ref[1, id1] += dv[NBR:]
         return 0
 
-    lax.fori_loop(0, spans, span, 0, unroll=4)
+    lax.fori_loop(0, spans, span, 0, unroll=8)
 
     def store(i, _):
         for j in range(2):
@@ -328,9 +328,10 @@
     batches = BATCHES
     batch = rows // batches
     loads = [pltpu.make_async_copy(kw_ref, w.at[0], w_sems.at[0]), pltpu.make_async_copy(vw_ref, w.at[1], w_sems.at[1])]
+    own_states = pltpu.make_async_copy(states_ref, st.at[place.head], w_sems.at[2])
+    own_states.start()
     for load in loads:
         load.start()
-    st[place.head] = states_ref[...]
     acc[...] = jnp.zeros_like(acc)
     greet(
         [place.ring(1), place.ring(-1), place.twin()]
@@ -433,6 +434,7 @@
         "relay": lambda b, j, i: gathers[b][j].relay(i),
         "swap": lambda i: (swap_first, swap_second)[i](),
     }
+    own_states.wait()
     waiting = list(loads)
     for name, *what in ORDER:
         if name in ("own", "other") and waiting:
@@ -466,7 +468,7 @@
             jax.ShapeDtypeStruct((2, seqs, rows, cols), jnp.bfloat16),
             jax.ShapeDtypeStruct((SIDE, SIDE, share, feats), jnp.bfloat16),
         ),
-        in_specs=[vmem, hbm, hbm],
+        in_specs=[hbm, hbm, hbm],
         out_specs=(vmem, vmem),
         scratch_shapes=[
             pltpu.VMEM((heads, rows, feats), jnp.bfloat16),
@@ -479,7 +481,7 @@
             dma((2, RING // 2, 2 * BATCHES)),
             dma((BATCHES, 2, 8)),
             dma((2, 2, 3)),
-            dma((2,)),
+            dma((3,)),
         ],
         compiler_params=pltpu.CompilerParams(
             collective_id=1, has_side_effects=True, vmem_limit_bytes=48 * MIB

time: 123 us -> 123 us (level)
  no operation moved by 1% of the time
where the time goes in v5:
time: 123 us
  Pallas kernels  119 us (97%)
  local copies, waits for them, and re-layouts  2.54 us (2%)
    pallas_call x1, Pallas kernels, pool(): pl.pallas_call(pool_kernel, out_shape=(jax.ShapeDtypeStruct((2, seqs, row...  57.2 us
    pallas_call x1, Pallas kernels, weight_grads(): pl.pallas_call(reduce_kernel, out_shape=(jax.ShapeDtypeStruct((feats, col...  50.5 us
    pallas_call x1, Pallas kernels, attend(): pl.pallas_call(attend_kernel, out_shape=(jax.ShapeDtypeStruct((rows, cols...  11.6 us
    unnamed x10, local copies, waits for them, and re-layouts  2.54 us

profile of v5, /device:TPU:2, one launch (start us, length us, event | category | flops | bytes accessed | tf_op | source)
XLA Modules:
  0.0 122.5 jit_solution(1571207658885768541)
XLA Ops:
  0.6 0.0 copy-start.2
  0.6 0.9 copy-done.2
  1.6 0.0 copy-start
  1.6 0.0 copy-start.1
  1.6 0.0 copy-start.3
  1.6 57.2 %pool.1 = (bf16[2,16,256,256]{3,2,1,0:T(8,128)(2,1)S(1)}, bf16[4,4,16,512]{3,2,1,0:T(8,128)(2,1)S(1)}) custom-call(bf16[256,512]{1,0:T(8,128)(2,1)S(1)} %copy-done.2, bf16[16,512,256]{2,1,0:T(8,128)(2,1)} %bitcast.10, bf16[16,512,256]{2,1,0:T(8,128)(2,1)} %bitcast.11), custom_call_target="tpu_custom_call" | custom-call | tf_op jit(solution)/shard_map/pool/pallas_call | solution.py:465
  58.8 0.0 copy-done
  58.9 0.0 copy-done.1
  58.9 0.0 copy-done.3
  58.9 11.6 %attend.1 = (bf16[1024,256]{1,0:T(8,128)(2,1)}, bf16[1024,256]{1,0:T(8,128)(2,1)}, bf16[2,32,128,256]{3,2,1,0:T(8,128)(2,1)S(1)}) custom-call(s32[2,16]{1,0:T(2,128)S(1)} %bitcast.9, bf16[1024,256]{1,0:T(8,128)(2,1)S(1)} %copy-done, bf16[1024,256]{1,0:T(8,128)(2,1)S(1)} %copy-done.1, bf16[2,32,128,256]{3,2,1,0:T(8,128)(2,1)S(1)} %bitcast.7), custom_call_target="tpu_custom_call" | custom-call | tf_op jit(solution)/shard_map/attend/pallas_call | solution.py:132
  70.4 50.5 %reduce_all.1 = (f32[512,256]{1,0:T(8,128)S(1)}, f32[512,256]{1,0:T(8,128)S(1)}) custom-call(bf16[2,16,256,256]{3,2,1,0:T(8,128)(2,1)S(1)} %bitcast.6, bf16[256,512]{1,0:T(8,128)(2,1)S(1)} %bitcast.8), custom_call_target="tpu_custom_call" | custom-call | tf_op jit(solution)/shard_map/reduce_all/pallas_call | solution.py:659
  121.0 0.8 copy.12
  121.7 0.8 copy.13
Async XLA Ops:
  0.6 1.0 copy-start.2
  1.6 57.3 %copy-start = (bf16[1024,256]{1,0:T(8,128)(2,1)S(1)}, bf16[1024,256]{1,0:T(8,128)(2,1)}, u32[]{:S(2)}) copy-start(bf16[1024,256]{1,0:T(8,128)(2,1)} %q_ref.1) | copy-start | bytes 1572868
  1.6 57.3 %copy-start.1 = (bf16[1024,256]{1,0:T(8,128)(2,1)S(1)}, bf16[1024,256]{1,0:T(8,128)(2,1)}, u32[]{:S(2)}) copy-start(bf16[1024,256]{1,0:T(8,128)(2,1)} %g_ref.1) | copy-start | bytes 1572868
  1.6 57.3 %copy-start.3 = (s32[16,2]{0,1:T(2,128)S(1)}, s32[16,2]{0,1:T(2,128)}, u32[]{:S(2)}) copy-start(s32[16,2]{0,1:T(2,128)} %param.10) | copy-start | bytes 388

commit v6 on v5

--- a/solution.py
+++ b/solution.py
@@ -70,7 +70,7 @@
     return jnp.dot(a, b, preferred_element_type=jnp.float32)
 
 
-def attend_kernel(ids_ref, q_ref, g_ref, kv_ref, ctx_ref, dq_ref, dkv_ref, acc_ref):
+def attend_kernel(ids_ref, q_ref, g_ref, kv_ref, ctx_out, dq_out, dkv_ref, acc_ref, ctx_ref, dq_ref, out_sems):
     cols = q_ref.shape[1]
     spans = q_ref.shape[0] // SPAN
     blocks = kv_ref.shape[1]
@@ -117,18 +117,27 @@
 
     lax.fori_loop(0, spans, span, 0, unroll=8)
 
+    writes = [
+        pltpu.make_async_copy(ctx_ref, ctx_out, out_sems.at[0]),
+        pltpu.make_async_copy(dq_ref, dq_out, out_sems.at[1]),
+    ]
+    for write in writes:
+        write.start()
+
     def store(i, _):
         for j in range(2):
             dkv_ref[j, i] = acc_ref[j, i].astype(jnp.bfloat16)
         return 0
 
     lax.fori_loop(0, blocks, store, 0)
+    for write in writes:
+        write.wait()
 
 
 def attend(ids, queries, grads, kv):
     rows, cols = queries.shape
     blocks = kv.shape[1] * kv.shape[2] // NBR
-    vmem = pl.BlockSpec(memory_space=pltpu.VMEM)
+    vmem, hbm = pl.BlockSpec(memory_space=pltpu.VMEM), pl.BlockSpec(memory_space=pltpu.HBM)
     context, query_grad, dkv = pl.pallas_call(
         attend_kernel,
         out_shape=(
@@ -137,8 +146,13 @@
             jax.ShapeDtypeStruct((2, blocks, NBR, cols), jnp.bfloat16),
         ),
         in_specs=[pl.BlockSpec(memory_space=pltpu.SMEM), vmem, vmem, vmem],
-        out_specs=(vmem, vmem, vmem),
-        scratch_shapes=[pltpu.VMEM((2, blocks, NBR, cols), jnp.float32)],
+        out_specs=(hbm, hbm, vmem),
+        scratch_shapes=[
+            pltpu.VMEM((2, blocks, NBR, cols), jnp.float32),
+            pltpu.VMEM((rows, cols), jnp.bfloat16),
+            pltpu.VMEM((rows, cols), jnp.bfloat16),
+            pltpu.SemaphoreType.DMA((2,)),
+        ],
         compiler_params=pltpu.CompilerParams(vmem_limit_bytes=40 * MIB),
         name="attend",
     )(ids, queries, grads, kv.reshape(2, blocks, NBR, cols))

time: 123 us -> 122 us (level)
  no operation moved by 1% of the time
where the time goes in v6:
time: 122 us
  Pallas kernels  118 us (97%)
  local copies, waits for them, and re-layouts  2.54 us (2%)
    pallas_call x1, Pallas kernels, pool(): pl.pallas_call(pool_kernel, out_shape=(jax.ShapeDtypeStruct((2, seqs, row...  57.2 us
    pallas_call x1, Pallas kernels, weight_grads(): pl.pallas_call(reduce_kernel, out_shape=(jax.ShapeDtypeStruct((feats, col...  50.5 us
    pallas_call x1, Pallas kernels, attend(): pl.pallas_call(attend_kernel, out_shape=(jax.ShapeDtypeStruct((rows, cols...  10.6 us
    unnamed x10, local copies, waits for them, and re-layouts  2.54 us

profile of v6, /device:TPU:2, one launch (start us, length us, event | category | flops | bytes accessed | tf_op | source)
XLA Modules:
  0.0 121.6 jit_solution(17018966883860386326)
XLA Ops:
  0.6 0.0 copy-start.2
  0.6 0.9 copy-done.2
  1.6 0.0 copy-start
  1.6 0.0 copy-start.1
  1.6 0.0 copy-start.3
  1.6 57.2 %pool.1 = (bf16[2,16,256,256]{3,2,1,0:T(8,128)(2,1)S(1)}, bf16[4,4,16,512]{3,2,1,0:T(8,128)(2,1)S(1)}) custom-call(bf16[256,512]{1,0:T(8,128)(2,1)S(1)} %copy-done.2, bf16[16,512,256]{2,1,0:T(8,128)(2,1)} %bitcast.10, bf16[16,512,256]{2,1,0:T(8,128)(2,1)} %bitcast.11), custom_call_target="tpu_custom_call" | custom-call | tf_op jit(solution)/shard_map/pool/pallas_call | solution.py:479
  58.8 0.0 copy-done
  58.9 0.0 copy-done.1
  58.9 0.0 copy-done.3
  58.9 10.6 %attend.1 = (bf16[1024,256]{1,0:T(8,128)(2,1)}, bf16[1024,256]{1,0:T(8,128)(2,1)}, bf16[2,32,128,256]{3,2,1,0:T(8,128)(2,1)S(1)}) custom-call(s32[2,16]{1,0:T(2,128)S(1)} %bitcast.9, bf16[1024,256]{1,0:T(8,128)(2,1)S(1)} %copy-done, bf16[1024,256]{1,0:T(8,128)(2,1)S(1)} %copy-done.1, bf16[2,32,128,256]{3,2,1,0:T(8,128)(2,1)S(1)} %bitcast.7), custom_call_target="tpu_custom_call" | custom-call | tf_op jit(solution)/shard_map/attend/pallas_call | solution.py:141
  69.5 50.5 %reduce_all.1 = (f32[512,256]{1,0:T(8,128)S(1)}, f32[512,256]{1,0:T(8,128)S(1)}) custom-call(bf16[2,16,256,256]{3,2,1,0:T(8,128)(2,1)S(1)} %bitcast.6, bf16[256,512]{1,0:T(8,128)(2,1)S(1)} %bitcast.8), custom_call_target="tpu_custom_call" | custom-call | tf_op jit(solution)/shard_map/reduce_all/pallas_call | solution.py:673
  120.0 0.8 copy.12
  120.8 0.8 copy.13
Async XLA Ops:
  0.6 1.0 copy-start.2
  1.6 57.3 %copy-start = (bf16[1024,256]{1,0:T(8,128)(2,1)S(1)}, bf16[1024,256]{1,0:T(8,128)(2,1)}, u32[]{:S(2)}) copy-start(bf16[1024,256]{1,0:T(8,128)(2,1)} %q_ref.1) | copy-start | bytes 1572868
  1.6 57.3 %copy-start.1 = (bf16[1024,256]{1,0:T(8,128)(2,1)S(1)}, bf16[1024,256]{1,0:T(8,128)(2,1)}, u32[]{:S(2)}) copy-start(bf16[1024,256]{1,0:T(8,128)(2,1)} %g_ref.1) | copy-start | bytes 1572868
  1.6 57.3 %copy-start.3 = (s32[16,2]{0,1:T(2,128)S(1)}, s32[16,2]{0,1:T(2,128)}, u32[]{:S(2)}) copy-start(s32[16,2]{0,1:T(2,128)} %param.10) | copy-start | bytes 388
